TPU v7x, 512 devices: a whole 4x8x8 slice. The times are simulated.
512 devices in a mesh: band: 64 (over y, z), lev: 8 (over x, core).
Axes of the slice: x: 4, y: 8, z: 8, core: 2. Of those that a mesh axis runs over, the one named last changes fastest.
Arguments:
- concentration: float32 [4, 8, 128, 256], P(None, 'lev', 'band'), may hold values from 0.1 to 2
- target: float32 [4, 8, 128, 256], P(None, 'lev', 'band'), may hold values from -6 to 6
- zonal_wind: float32 [8, 128, 256], P('lev', 'band'), may hold values from -0.6 to 0.6
- merid_wind: float32 [8, 128, 256], P('lev', 'band'), may hold values from -0.6 to 0.6
- sea_mask: int32 [128, 256], P('band'), may hold values 0 or 1
- first_weight: float32 [2, 20, 128], replicated, may hold values from -1.25 to 1.25
- first_bias: float32 [2, 128], replicated, may hold values from -3 to 3
- middle_weight: float32 [2, 128, 128], replicated, may hold values from -0.5 to 0.5
- middle_bias: float32 [2, 128], replicated, may hold values from -3 to 3
- last_weight: float32 [2, 4, 128], replicated, may hold values from -0.125 to 0.125
- last_bias: float32 [2, 4], replicated, may hold values from -0.6 to 0.6
Outputs:
- final_field: float32 [4, 8, 128, 256], P(None, 'lev', 'band')
- first_weight_grad: float32 [2, 20, 128], replicated
- first_bias_grad: float32 [2, 128], replicated
- middle_weight_grad: float32 [2, 128, 128], replicated
- middle_bias_grad: float32 [2, 128], replicated
- last_weight_grad: float32 [2, 4, 128], replicated
- last_bias_grad: float32 [2, 4], replicated
Inputs may be any that keep to these rules, and one draw needn't show every extreme that they name: `sea_mask`: 1 marks a sea cell, 0 a land cell.
All inputs are finite; a program needn't handle non-finite values. No bound on the sum of `sea_mask` on one device may be relied on, other than what follows from the above.
Results may differ from a plain program's by a relative error of at most 0.00013.
Values sent between devices are 32-bit elements; how exact they have to be, the bound alone decides.
A program may use at most 64 MiB of HBM per device.

v0:
```python
import math

import jax
import jax.numpy as jnp
from jax import lax
from jax.sharding import PartitionSpec as P

STEPS = 3


stencil_base = (-1.0 / 12.0, 7.0 / 12.0, 7.0 / 12.0, -1.0 / 12.0)


def cut_along(array, direction, start, length):
    return lax.slice_in_dim(array, start, start + length, axis=direction)


def pad_along(array, direction, width):
    widths = [(0, 0)] * array.ndim
    widths[direction] = (width, width)
    return jnp.pad(array, widths)


def face_flux(network, stencil, courant, mask_low, mask_high):
    w_first, b_first, w_second, b_second, w_last, b_last = network
    face_shape = courant.shape
    columns = courant.size
    nbins = stencil.shape[1]
    features = jnp.concatenate(
        [
            stencil.reshape(4 * nbins, columns),
            courant.reshape(1, columns),
            (courant * courant).reshape(1, columns),
            mask_low.reshape(1, columns),
            mask_high.reshape(1, columns),
        ],
        0,
    )
    hidden_one = jnp.tanh(
        jnp.dot(w_first.T, features, precision=lax.Precision.HIGHEST) + b_first[:, None]
    )
    hidden_two = jnp.tanh(
        jnp.dot(w_second.T, hidden_one, precision=lax.Precision.HIGHEST) + b_second[:, None]
    )
    output = jnp.dot(w_last, hidden_two, precision=lax.Precision.HIGHEST) + b_last[:, None]
    correction = output - jnp.mean(output, 0, keepdims=True)
    weights_face = jnp.asarray(stencil_base, jnp.float32)[:, None] + correction
    face_value = jnp.sum(weights_face.reshape((4, 1) + face_shape) * stencil, 0)
    return courant[None] * face_value


def advance(network, padded, wind_padded, mask_padded, direction):
    length = padded.shape[direction] - 4
    stencil = jnp.stack([cut_along(padded, direction, offset, length + 1) for offset in range(4)])
    courant = 0.5 * (
        cut_along(wind_padded, direction - 1, 0, length + 1)
        + cut_along(wind_padded, direction - 1, 1, length + 1)
    )
    mask_low = cut_along(mask_padded, direction - 1, 0, length + 1)
    mask_high = cut_along(mask_padded, direction - 1, 1, length + 1)
    fluxes = face_flux(network, stencil, courant, mask_low, mask_high)
    centre = cut_along(padded, direction, 2, length)
    return centre - (
        cut_along(fluxes, direction, 1, length) - cut_along(fluxes, direction, 0, length)
    )


def to_columns(field):
    return lax.all_to_all(field, "band", split_axis=3, concat_axis=2, tiled=True)


def to_rows(field):
    return lax.all_to_all(field, "band", split_axis=2, concat_axis=3, tiled=True)


def on_device(
    concentration,
    target,
    zonal_wind,
    merid_wind,
    sea_mask,
    first_weight,
    first_bias,
    middle_weight,
    middle_bias,
    last_weight,
    last_bias,
):
    params = (first_weight, first_bias, middle_weight, middle_bias, last_weight, last_bias)
    zonal_net = tuple((member[0] for member in params))
    merid_net = tuple((member[1] for member in params))
    bins_here, levels_here, row_count, col_count = concentration.shape
    total_cells = (
        bins_here
        * levels_here
        * row_count
        * col_count
        * lax.axis_size("band")
        * lax.axis_size("lev")
    )
    loss_scale = 1.0 / math.sqrt(total_cells)
    sea_field = sea_mask.astype(jnp.float32)[None]
    wind_zonal = pad_along(zonal_wind, 2, 1)
    mask_zonal = pad_along(sea_field, 2, 1)
    stacked = jnp.concatenate([merid_wind, sea_field], 0)
    columns_data = lax.all_to_all(stacked, "band", split_axis=2, concat_axis=1, tiled=True)
    wind_merid = pad_along(columns_data[:levels_here], 1, 1)
    mask_merid = pad_along(columns_data[levels_here:], 1, 1)

    def zonal_sweep(network, padded):
        return advance(network, padded, wind_zonal, mask_zonal, 3)

    def merid_sweep(network, padded):
        return advance(network, padded, wind_merid, mask_merid, 2)

    pullbacks = []
    field = concentration
    for step_number in range(STEPS):
        field, zonal_back = jax.vjp(zonal_sweep, zonal_net, pad_along(field, 3, 2))
        moved, merid_back = jax.vjp(merid_sweep, merid_net, pad_along(to_columns(field), 2, 2))
        field = to_rows(moved)
        pullbacks.append((zonal_back, merid_back))
    cotangent = (field - target) * loss_scale
    sums = tuple((jnp.zeros_like(member) for member in params))
    for step_number in reversed(range(STEPS)):
        zonal_back, merid_back = pullbacks[step_number]
        merid_grads, padded_grad = merid_back(to_columns(cotangent))
        cotangent = to_rows(padded_grad[:, :, 2:-2])
        zonal_grads, padded_grad = zonal_back(cotangent)
        cotangent = padded_grad[:, :, :, 2:-2]
        step_grads = tuple(
            (
                jnp.stack([zonal_part, merid_part])
                for zonal_part, merid_part in zip(zonal_grads, merid_grads)
            )
        )
        sums = tuple((earlier + latest for earlier, latest in zip(sums, step_grads)))
    sums = lax.psum((sums[0], sums[1], sums[2], sums[3], sums[4], sums[5]), ("band", "lev"))
    return (field, sums[0], sums[1], sums[2], sums[3], sums[4], sums[5])


def solution(mesh):
    return jax.shard_map(
        on_device,
        mesh=mesh,
        in_specs=(
            P(None, "lev", "band", None),
            P(None, "lev", "band", None),
            P("lev", "band", None),
            P("lev", "band", None),
            P("band", None),
            P(),
            P(),
            P(),
            P(),
            P(),
            P(),
        ),
        out_specs=(P(None, "lev", "band", None), P(), P(), P(), P(), P(), P()),
        check_vma=False,
    )
```

profile of v0, /device:TPU:1, one launch (start us, length us, event | category | flops | bytes accessed | tf_op | source)
XLA Modules:
  0.0 649.2 jit_solution(2578516520645093349)
XLA Ops:
  9.5 17.3 %all-to-all-start.1 = ((f32[2,2,256]{1,0,2:T(2,128)}), f32[2,2,256]{1,0,2:T(2,128)S(1)}, u32[]{:S(2)}, u32[]{:S(2)}) async-start(f32[2,2,256]{1,0,2:T(2,128)} %copy.634), calls=%async_computation.1 | async-start | bytes 524288 | tf_op jit(solution)/shard_map/all_to_all | solution.py:106
  36.5 3.0 all-to-all-done.1
  39.6 9.1 %all-to-all-start = ((f32[4,1,2,256]{0,2,1,3:T(2,128)}), f32[4,1,2,256]{0,2,1,3:T(2,128)S(1)}, u32[]{:S(2)}, u32[]{:S(2)}) async-start(f32[4,1,2,256]{0,2,1,3:T(2,128)} %copy.631), calls=%async_computation | async-start | bytes 524288 | tf_op jit(solution)/shard_map/all_to_all | solution.py:69
  50.4 10.8 %all-to-all-done = f32[4,1,2,256]{0,2,1,3:T(2,128)S(1)} async-done(((f32[4,1,2,256]{0,2,1,3:T(2,128)}), f32[4,1,2,256]{0,2,1,3:T(2,128)S(1)}, u32[]{:S(2)}, u32[]{:S(2)}) %all-to-all-start) | async-done | bytes 8224 | tf_op jit(solution)/shard_map/all_to_all | solution.py:69
  66.5 18.4 %all_to_all.231 = f32[4,1,128,4]{3,0,1,2:T(4,128)S(1)} all-to-all(f32[4,1,128,4]{3,0,1,2:T(4,128)S(1)} %copy.642), channel_id=1, replica_groups=mesh['band'=64,'lev'=8] {'band'}, dimensions={2} | all-to-all | bytes 16384 | tf_op jit(solution)/shard_map/all_to_all | solution.py:73
  88.9 18.4 %all_to_all.232 = f32[4,1,2,256]{0,2,1,3:T(2,128)S(1)} all-to-all(f32[4,1,2,256]{0,2,1,3:T(2,128)S(1)} %copy.646), channel_id=1, replica_groups=mesh['band'=64,'lev'=8] {'band'}, dimensions={3} | all-to-all | bytes 16384 | tf_op jit(solution)/shard_map/all_to_all | solution.py:69
  110.4 1.5 concatenate.121
  111.9 1.3 fusion.8
  113.3 1.2 fusion.2
  115.2 1.0 fusion.101
  117.3 18.4 %all_to_all.233 = f32[4,1,128,4]{3,0,1,2:T(4,128)S(1)} all-to-all(f32[4,1,128,4]{3,0,1,2:T(4,128)S(1)} %copy.651), channel_id=1, replica_groups=mesh['band'=64,'lev'=8] {'band'}, dimensions={2} | all-to-all | bytes 16384 | tf_op jit(solution)/shard_map/all_to_all | solution.py:73
  139.6 18.4 %all_to_all.234 = f32[4,1,2,256]{0,2,1,3:T(2,128)S(1)} all-to-all(f32[4,1,2,256]{0,2,1,3:T(2,128)S(1)} %copy.655), channel_id=1, replica_groups=mesh['band'=64,'lev'=8] {'band'}, dimensions={3} | all-to-all | bytes 16384 | tf_op jit(solution)/shard_map/all_to_all | solution.py:69
  160.7 1.5 slice_bitcast_fusion.15
  162.2 1.1 pad_maximum_fusion.2
  163.3 2.2 reshape.1580
  165.5 2.7 concatenate.123
  168.2 1.5 fusion.6
  169.7 1.2 fusion
  171.6 1.0 fusion.103
  172.7 1.3 add_bitcast_fusion
  174.0 1.6 mul.546
  175.5 1.9 multiply_reduce_fusion
  177.4 1.7 copy.716
  179.9 1.4 fusion.44
  181.2 1.6 copy.660
  182.8 18.8 %all_to_all.235 = f32[4,1,128,4]{3,0,1,2:T(4,128)S(1)} all-to-all(f32[4,1,128,4]{3,0,1,2:T(4,128)} %copy.660), channel_id=1, replica_groups=mesh['band'=64,'lev'=8] {'band'}, dimensions={2} | all-to-all | bytes 16384 | tf_op jit(solution)/shard_map/all_to_all | solution.py:73
  202.4 1.7 all_to_all.193
  204.1 1.3 fusion.50
  205.5 1.6 copy.664
  207.0 18.1 %all_to_all.236 = f32[4,1,2,256]{0,2,1,3:T(2,128)} all-to-all(f32[4,1,2,256]{0,2,1,3:T(2,128)} %copy.664), channel_id=1, replica_groups=mesh['band'=64,'lev'=8] {'band'}, dimensions={3} | all-to-all | bytes 16384 | tf_op jit(solution)/shard_map/all_to_all | solution.py:69
  225.2 2.6 copy.711
  227.8 1.9 copy.666
  229.7 1.7 copy.667
  232.0 1.4 multiply_bitcast_fusion.2
  233.4 1.6 copy.669
  235.0 1.9 multiply_reduce_fusion.7
  237.6 1.7 reshape.1587
  239.3 1.6 fusion.90
  241.1 1.2 fusion.110
  242.2 1.3 convolution_bitcast_fusion.4
  243.6 1.1 fusion.104
  246.6 1.1 reshape.1581
  247.7 1.1 bitcast_add_fusion.2
  250.9 4.7 all-to-all-start.8
  255.6 1.5 convolution_bitcast_fusion.21
  257.2 11.0 %all-to-all-done.8 = f32[4,1,128,4]{3,0,1,2:T(4,128)S(1)} async-done(((f32[4,1,128,4]{3,0,1,2:T(4,128)}), f32[4,1,128,4]{3,0,1,2:T(4,128)S(1)}, u32[]{:S(2)}, u32[]{:S(2)}) %all-to-all-start.8) | async-done | bytes 8224 | tf_op jit(solution)/shard_map/all_to_all | solution.py:73
  269.6 1.2 fusion.111
  270.8 1.3 convolution_bitcast_fusion.5
  272.1 1.1 fusion.105
  275.7 5.0 all-to-all-start.9
  281.5 11.8 %all-to-all-done.9 = f32[4,1,2,256]{0,2,1,3:T(2,128)S(1)} async-done(((f32[4,1,2,256]{0,2,1,3:T(2,128)}), f32[4,1,2,256]{0,2,1,3:T(2,128)S(1)}, u32[]{:S(2)}, u32[]{:S(2)}) %all-to-all-start.9) | async-done | bytes 8224 | tf_op jit(solution)/shard_map/all_to_all | solution.py:69
  293.3 1.0 copy.712
  298.0 1.2 fusion.112
  299.1 1.3 convolution_bitcast_fusion.2
  300.5 1.1 fusion.106
  305.4 4.7 all-to-all-start.10
  310.4 12.3 %all-to-all-done.10 = f32[4,1,128,4]{3,0,1,2:T(4,128)S(1)} async-done(((f32[4,1,128,4]{3,0,1,2:T(4,128)}), f32[4,1,128,4]{3,0,1,2:T(4,128)S(1)}, u32[]{:S(2)}, u32[]{:S(2)}) %all-to-all-start.10) | async-done | bytes 8224 | tf_op jit(solution)/shard_map/all_to_all | solution.py:73
  327.3 4.8 all-to-all-start.11
  332.3 12.3 %all-to-all-done.11 = f32[4,1,2,256]{0,2,1,3:T(2,128)S(1)} async-done(((f32[4,1,2,256]{0,2,1,3:T(2,128)}), f32[4,1,2,256]{0,2,1,3:T(2,128)S(1)}, u32[]{:S(2)}, u32[]{:S(2)}) %all-to-all-start.11) | async-done | bytes 8224 | tf_op jit(solution)/shard_map/all_to_all | solution.py:69
  351.7 4.7 all-to-all-start.12
  356.7 12.2 %all-to-all-done.12 = f32[4,1,128,4]{3,0,1,2:T(4,128)S(1)} async-done(((f32[4,1,128,4]{3,0,1,2:T(4,128)}), f32[4,1,128,4]{3,0,1,2:T(4,128)S(1)}, u32[]{:S(2)}, u32[]{:S(2)}) %all-to-all-start.12) | async-done | bytes 8224 | tf_op jit(solution)/shard_map/all_to_all | solution.py:73
  373.4 104.7 %all-reduce.47 = (f32[2,20,128]{2,1,0:T(8,128)S(1)}, f32[2,128]{1,0:T(2,128)}, f32[2,128]{1,0:T(2,128)}, f32[2,4,128]{2,1,0:T(4,128)}, f32[2,4]{1,0:T(2,128)}) all-reduce(f32[2,20,128]{2,1,0:T(8,128)S(1)} %fusion.37, f32[2,128]{1,0:T(2,128)S(1)} %get-tuple-element.216, ...), channel_id=1, replica_groups=mesh['band'=64,'lev'=8] {'band','lev'}, use_global_device_ids=true, to_apply=%region_24.25 | all-reduce | flops 6664 | bytes 53312 | tf_op jit(solution)/shard_map/psum | solution.py:138
  478.7 161.8 %all-reduce.50.cloned.1.call-done = f32[2,128,128]{2,1,0:T(8,128)} async-done(((f32[2,128,128]{2,1,0:T(8,128)}), f32[2,128,128]{2,1,0:T(8,128)}) %all-reduce.50.cloned.1.call-update) | async-done | bytes 131088 | tf_op jit(solution)/shard_map/psum | solution.py:138
  640.6 1.6 copy.764
  (477 shorter events, 69.7 us)
Async XLA Ops:
  7.2 26.5 %copy-start = (f32[2,128,128]{2,1,0:T(8,128)S(1)}, f32[2,128,128]{2,1,0:T(8,128)}, u32[]{:S(2)}) copy-start(f32[2,128,128]{2,1,0:T(8,128)} %param.24) | copy-start | bytes 393220
  8.6 26.4 %copy-start.73 = (f32[2,4,128]{2,1,0:T(4,128)S(1)}, f32[2,4,128]{2,1,0:T(4,128)}, u32[]{:S(2)}) copy-start(f32[2,4,128]{2,1,0:T(4,128)} %param.26) | copy-start | bytes 12292
  9.5 25.9 %copy-start.100 = (f32[4]{0:T(128)S(1)}, f32[4]{0:T(128)}, u32[]{:S(2)}) copy-start(f32[4]{0:T(128)} %constant.29.clone) | copy-start | bytes 52
  9.5 26.1 %copy-start.82 = (f32[4,1,2,256]{3,2,1,0:T(2,128)S(1)}, f32[4,1,2,256]{3,2,1,0:T(2,128)}, u32[]{:S(2)}) copy-start(f32[4,1,2,256]{3,2,1,0:T(2,128)} %param.17) | copy-start | bytes 24580
  9.5 30.1 %all-to-all-start.1 = ((f32[2,2,256]{1,0,2:T(2,128)}), f32[2,2,256]{1,0,2:T(2,128)S(1)}, u32[]{:S(2)}, u32[]{:S(2)}) async-start(f32[2,2,256]{1,0,2:T(2,128)} %copy.634), calls=%async_computation.1 | async-start | bytes 524288 | tf_op jit(solution)/shard_map/all_to_all | solution.py:106
  27.6 12.0 %copy-start.49 = (f32[1,4,1,2,257]{4,3,1,2,0:T(2,128)}, f32[1,4,1,2,257]{4,3,1,2,0:T(2,128)S(1)}, u32[]{:S(2)}) copy-start(f32[1,4,1,2,257]{4,3,1,2,0:T(2,128)S(1)} %slice_bitcast_fusion.43) | copy-start | bytes 24676
  29.1 34.0 %copy-start.103 = (f32[128]{0:T(128)}, f32[128]{0:T(128)S(1)}, u32[]{:S(2)}) copy-start(f32[128]{0:T(128)S(1)} %get-tuple-element.178) | copy-start | bytes 1540
  29.1 56.4 %copy-start.105 = (f32[128]{0:T(128)}, f32[128]{0:T(128)S(1)}, u32[]{:S(2)}) copy-start(f32[128]{0:T(128)S(1)} %get-tuple-element.179) | copy-start | bytes 1540
  29.9 34.0 %copy-start.111 = (f32[128]{0:T(128)}, f32[128]{0:T(128)S(1)}, u32[]{:S(2)}) copy-start(f32[128]{0:T(128)S(1)} %get-tuple-element.176) | copy-start | bytes 1540
  29.9 56.3 %copy-start.112 = (f32[128]{0:T(128)}, f32[128]{0:T(128)S(1)}, u32[]{:S(2)}) copy-start(f32[128]{0:T(128)S(1)} %get-tuple-element.177) | copy-start | bytes 1540
  30.6 33.8 %copy-start.104 = (f32[4]{0:T(128)}, f32[4]{0:T(128)S(1)}, u32[]{:S(2)}) copy-start(f32[4]{0:T(128)S(1)} %get-tuple-element.174) | copy-start | bytes 52
  30.6 56.1 %copy-start.107 = (f32[4]{0:T(128)}, f32[4]{0:T(128)S(1)}, u32[]{:S(2)}) copy-start(f32[4]{0:T(128)S(1)} %get-tuple-element.175) | copy-start | bytes 52
  30.7 54.7 %copy-start.91 = (f32[1,514]{1,0:T(1,128)}, f32[1,514]{1,0:T(1,128)S(1)}, u32[]{:S(2)}) copy-start(f32[1,514]{1,0:T(1,128)S(1)} %reshape.1571) | copy-start | bytes 6172
  30.8 54.6 %copy-start.93 = (f32[1,514]{1,0:T(1,128)}, f32[1,514]{1,0:T(1,128)S(1)}, u32[]{:S(2)}) copy-start(f32[1,514]{1,0:T(1,128)S(1)} %reshape.1570) | copy-start | bytes 6172
  31.7 53.7 %copy-start.95 = (f32[1,514]{1,0:T(1,128)}, f32[1,514]{1,0:T(1,128)S(1)}, u32[]{:S(2)}) copy-start(f32[1,514]{1,0:T(1,128)S(1)} %reshape.1569) | copy-start | bytes 6172
  31.8 53.6 %copy-start.97 = (f32[1,514]{1,0:T(1,128)}, f32[1,514]{1,0:T(1,128)S(1)}, u32[]{:S(2)}) copy-start(f32[1,514]{1,0:T(1,128)S(1)} %reshape.1568) | copy-start | bytes 6172
  32.7 52.8 %copy-start.43 = (f32[1,20,128]{2,0,1:T(1,128)}, f32[1,20,128]{2,0,1:T(1,128)S(1)}, u32[]{:S(2)}) copy-start(f32[1,20,128]{2,0,1:T(1,128)S(1)} %get-tuple-element.154) | copy-start | bytes 30724
  32.8 6.8 %copy-start.51 = (f32[1,4,1,2,257]{4,3,1,2,0:T(2,128)}, f32[1,4,1,2,257]{4,3,1,2,0:T(2,128)S(1)}, u32[]{:S(2)}) copy-start(f32[1,4,1,2,257]{4,3,1,2,0:T(2,128)S(1)} %get-tuple-element.155) | copy-start | bytes 24676
  32.8 6.8 %copy-start.53 = (f32[1,4,1,2,257]{4,3,1,2,0:T(2,128)}, f32[1,4,1,2,257]{4,3,1,2,0:T(2,128)S(1)}, u32[]{:S(2)}) copy-start(f32[1,4,1,2,257]{4,3,1,2,0:T(2,128)S(1)} %get-tuple-element.156) | copy-start | bytes 24676
  32.8 6.8 %copy-start.55 = (f32[1,4,1,2,257]{4,3,1,2,0:T(2,128)}, f32[1,4,1,2,257]{4,3,1,2,0:T(2,128)S(1)}, u32[]{:S(2)}) copy-start(f32[1,4,1,2,257]{4,3,1,2,0:T(2,128)S(1)} %get-tuple-element.157) | copy-start | bytes 24676
  39.6 21.6 %all-to-all-start = ((f32[4,1,2,256]{0,2,1,3:T(2,128)}), f32[4,1,2,256]{0,2,1,3:T(2,128)S(1)}, u32[]{:S(2)}, u32[]{:S(2)}) async-start(f32[4,1,2,256]{0,2,1,3:T(2,128)} %copy.631), calls=%async_computation | async-start | bytes 524288 | tf_op jit(solution)/shard_map/all_to_all | solution.py:69
  50.0 13.1 %copy-start.87 = (f32[1,516]{1,0:T(1,128)}, f32[1,516]{1,0:T(1,128)S(1)}, u32[]{:S(2)}) copy-start(f32[1,516]{1,0:T(1,128)S(1)} %reshape.1574) | copy-start | bytes 6196
  50.1 13.0 %copy-start.88 = (f32[1,516]{1,0:T(1,128)}, f32[1,516]{1,0:T(1,128)S(1)}, u32[]{:S(2)}) copy-start(f32[1,516]{1,0:T(1,128)S(1)} %reshape.1573) | copy-start | bytes 6196
  50.3 12.8 %copy-start.89 = (f32[1,516]{1,0:T(1,128)}, f32[1,516]{1,0:T(1,128)S(1)}, u32[]{:S(2)}) copy-start(f32[1,516]{1,0:T(1,128)S(1)} %reshape.1576) | copy-start | bytes 6196
  50.4 12.7 %copy-start.90 = (f32[1,516]{1,0:T(1,128)}, f32[1,516]{1,0:T(1,128)S(1)}, u32[]{:S(2)}) copy-start(f32[1,516]{1,0:T(1,128)S(1)} %reshape.1575) | copy-start | bytes 6196
  110.4 5.9 copy-start.101
  116.6 19.5 %copy-start.92 = (f32[1,514]{1,0:T(1,128)S(1)}, f32[1,514]{1,0:T(1,128)}, u32[]{:S(2)}) copy-start(f32[1,514]{1,0:T(1,128)} %copy-done.91) | copy-start | bytes 6172
  116.6 19.5 %copy-start.94 = (f32[1,514]{1,0:T(1,128)S(1)}, f32[1,514]{1,0:T(1,128)}, u32[]{:S(2)}) copy-start(f32[1,514]{1,0:T(1,128)} %copy-done.93) | copy-start | bytes 6172
  116.7 19.5 %copy-start.96 = (f32[1,514]{1,0:T(1,128)S(1)}, f32[1,514]{1,0:T(1,128)}, u32[]{:S(2)}) copy-start(f32[1,514]{1,0:T(1,128)} %copy-done.95) | copy-start | bytes 6172
  116.7 19.5 %copy-start.98 = (f32[1,514]{1,0:T(1,128)S(1)}, f32[1,514]{1,0:T(1,128)}, u32[]{:S(2)}) copy-start(f32[1,514]{1,0:T(1,128)} %copy-done.97) | copy-start | bytes 6172
  116.7 19.5 %copy-start.44 = (f32[1,20,128]{2,0,1:T(1,128)S(1)}, f32[1,20,128]{2,0,1:T(1,128)}, u32[]{:S(2)}) copy-start(f32[1,20,128]{2,0,1:T(1,128)} %copy-done.43) | copy-start | bytes 30724
  116.7 19.5 %copy-start.106 = (f32[128]{0:T(128)S(1)}, f32[128]{0:T(128)}, u32[]{:S(2)}) copy-start(f32[128]{0:T(128)} %copy-done.105) | copy-start | bytes 1540
  117.1 19.8 %copy-start.113 = (f32[128]{0:T(128)S(1)}, f32[128]{0:T(128)}, u32[]{:S(2)}) copy-start(f32[128]{0:T(128)} %copy-done.112) | copy-start | bytes 1540
  236.9 5.3 copy-start.25
  249.8 5.8 copy-start.13
  249.9 18.6 %copy-start.66 = (f32[1,4,1,2,257]{4,3,1,2,0:T(2,128)S(1)}, f32[1,4,1,2,257]{4,3,1,2,0:T(2,128)}, u32[]{:S(2)}) copy-start(f32[1,4,1,2,257]{4,3,1,2,0:T(2,128)} %copy-done.65) | copy-start | bytes 24676
  249.9 18.6 %copy-start.68 = (f32[1,4,1,2,257]{4,3,1,2,0:T(2,128)S(1)}, f32[1,4,1,2,257]{4,3,1,2,0:T(2,128)}, u32[]{:S(2)}) copy-start(f32[1,4,1,2,257]{4,3,1,2,0:T(2,128)} %copy-done.67) | copy-start | bytes 24676
  249.9 18.6 %copy-start.70 = (f32[1,4,1,2,257]{4,3,1,2,0:T(2,128)S(1)}, f32[1,4,1,2,257]{4,3,1,2,0:T(2,128)}, u32[]{:S(2)}) copy-start(f32[1,4,1,2,257]{4,3,1,2,0:T(2,128)} %copy-done.69) | copy-start | bytes 24676
  250.0 18.6 %copy-start.72 = (f32[1,4,1,2,257]{4,3,1,2,0:T(2,128)S(1)}, f32[1,4,1,2,257]{4,3,1,2,0:T(2,128)}, u32[]{:S(2)}) copy-start(f32[1,4,1,2,257]{4,3,1,2,0:T(2,128)} %copy-done.71) | copy-start | bytes 24676
  250.0 19.6 %copy-start.10 = (f32[514,128]{1,0:T(8,128)S(1)}, f32[514,128]{1,0:T(8,128)}, u32[]{:S(2)}) copy-start(f32[514,128]{1,0:T(8,128)} %copy-done.9) | copy-start | bytes 789508
  250.0 19.6 %copy-start.76 = (f32[2,4,128]{2,1,0:T(4,128)S(1)}, f32[2,4,128]{2,1,0:T(4,128)}, u32[]{:S(2)}) copy-start(f32[2,4,128]{2,1,0:T(4,128)} %param.26) | copy-start | bytes 12292
  250.9 19.9 %copy-start.23 = (f32[514,128]{1,0:T(8,128)S(1)}, f32[514,128]{1,0:T(8,128)}, u32[]{:S(2)}) copy-start(f32[514,128]{1,0:T(8,128)} %copy-done.22) | copy-start | bytes 789508
  250.9 17.3 %all-to-all-start.8 = ((f32[4,1,128,4]{3,0,1,2:T(4,128)}), f32[4,1,128,4]{3,0,1,2:T(4,128)S(1)}, u32[]{:S(2)}, u32[]{:S(2)}) async-start(f32[4,1,128,4]{3,0,1,2:T(4,128)} %copy.671), calls=%async_computation.8 | async-start | bytes 524288 | tf_op jit(solution)/shard_map/all_to_all | solution.py:73
  268.4 4.8 copy-start.41
  275.7 17.6 %all-to-all-start.9 = ((f32[4,1,2,256]{0,2,1,3:T(2,128)}), f32[4,1,2,256]{0,2,1,3:T(2,128)S(1)}, u32[]{:S(2)}, u32[]{:S(2)}) async-start(f32[4,1,2,256]{0,2,1,3:T(2,128)} %copy.677), calls=%async_computation.9 | async-start | bytes 524288 | tf_op jit(solution)/shard_map/all_to_all | solution.py:69
  304.3 5.8 copy-start.86
  304.3 5.8 copy-start.102
  304.4 18.6 %copy-start.58 = (f32[1,4,1,2,257]{4,3,1,2,0:T(2,128)S(1)}, f32[1,4,1,2,257]{4,3,1,2,0:T(2,128)}, u32[]{:S(2)}) copy-start(f32[1,4,1,2,257]{4,3,1,2,0:T(2,128)} %copy-done.57) | copy-start | bytes 24676
  304.4 18.6 %copy-start.60 = (f32[1,4,1,2,257]{4,3,1,2,0:T(2,128)S(1)}, f32[1,4,1,2,257]{4,3,1,2,0:T(2,128)}, u32[]{:S(2)}) copy-start(f32[1,4,1,2,257]{4,3,1,2,0:T(2,128)} %copy-done.59) | copy-start | bytes 24676
  304.4 18.6 %copy-start.62 = (f32[1,4,1,2,257]{4,3,1,2,0:T(2,128)S(1)}, f32[1,4,1,2,257]{4,3,1,2,0:T(2,128)}, u32[]{:S(2)}) copy-start(f32[1,4,1,2,257]{4,3,1,2,0:T(2,128)} %copy-done.61) | copy-start | bytes 24676
  304.5 18.6 %copy-start.64 = (f32[1,4,1,2,257]{4,3,1,2,0:T(2,128)S(1)}, f32[1,4,1,2,257]{4,3,1,2,0:T(2,128)}, u32[]{:S(2)}) copy-start(f32[1,4,1,2,257]{4,3,1,2,0:T(2,128)} %copy-done.63) | copy-start | bytes 24676
  304.5 19.0 %copy-start.6 = (f32[514,128]{1,0:T(8,128)S(1)}, f32[514,128]{1,0:T(8,128)}, u32[]{:S(2)}) copy-start(f32[514,128]{1,0:T(8,128)} %copy-done.5) | copy-start | bytes 789508
  304.5 19.0 %copy-start.77 = (f32[2,4,128]{2,1,0:T(4,128)S(1)}, f32[2,4,128]{2,1,0:T(4,128)}, u32[]{:S(2)}) copy-start(f32[2,4,128]{2,1,0:T(4,128)} %param.26) | copy-start | bytes 12292
  305.3 18.8 %copy-start.19 = (f32[514,128]{1,0:T(8,128)S(1)}, f32[514,128]{1,0:T(8,128)}, u32[]{:S(2)}) copy-start(f32[514,128]{1,0:T(8,128)} %copy-done.18) | copy-start | bytes 789508
  305.4 17.3 %all-to-all-start.10 = ((f32[4,1,128,4]{3,0,1,2:T(4,128)}), f32[4,1,128,4]{3,0,1,2:T(4,128)S(1)}, u32[]{:S(2)}, u32[]{:S(2)}) async-start(f32[4,1,128,4]{3,0,1,2:T(4,128)} %copy.684), calls=%async_computation.10 | async-start | bytes 524288 | tf_op jit(solution)/shard_map/all_to_all | solution.py:73
  327.3 17.3 %all-to-all-start.11 = ((f32[4,1,2,256]{0,2,1,3:T(2,128)}), f32[4,1,2,256]{0,2,1,3:T(2,128)S(1)}, u32[]{:S(2)}, u32[]{:S(2)}) async-start(f32[4,1,2,256]{0,2,1,3:T(2,128)} %copy.690), calls=%async_computation.11 | async-start | bytes 524288 | tf_op jit(solution)/shard_map/all_to_all | solution.py:69
  350.7 18.5 %copy-start.50 = (f32[1,4,1,2,257]{4,3,1,2,0:T(2,128)S(1)}, f32[1,4,1,2,257]{4,3,1,2,0:T(2,128)}, u32[]{:S(2)}) copy-start(f32[1,4,1,2,257]{4,3,1,2,0:T(2,128)} %copy-done.49) | copy-start | bytes 24676
  350.7 18.5 %copy-start.52 = (f32[1,4,1,2,257]{4,3,1,2,0:T(2,128)S(1)}, f32[1,4,1,2,257]{4,3,1,2,0:T(2,128)}, u32[]{:S(2)}) copy-start(f32[1,4,1,2,257]{4,3,1,2,0:T(2,128)} %copy-done.51) | copy-start | bytes 24676
  350.7 18.5 %copy-start.54 = (f32[1,4,1,2,257]{4,3,1,2,0:T(2,128)S(1)}, f32[1,4,1,2,257]{4,3,1,2,0:T(2,128)}, u32[]{:S(2)}) copy-start(f32[1,4,1,2,257]{4,3,1,2,0:T(2,128)} %copy-done.53) | copy-start | bytes 24676
  350.8 18.5 %copy-start.56 = (f32[1,4,1,2,257]{4,3,1,2,0:T(2,128)S(1)}, f32[1,4,1,2,257]{4,3,1,2,0:T(2,128)}, u32[]{:S(2)}) copy-start(f32[1,4,1,2,257]{4,3,1,2,0:T(2,128)} %copy-done.55) | copy-start | bytes 24676
  350.8 19.0 %copy-start.2 = (f32[514,128]{1,0:T(8,128)S(1)}, f32[514,128]{1,0:T(8,128)}, u32[]{:S(2)}) copy-start(f32[514,128]{1,0:T(8,128)} %copy-done.1) | copy-start | bytes 789508
  351.7 18.8 %copy-start.15 = (f32[514,128]{1,0:T(8,128)S(1)}, f32[514,128]{1,0:T(8,128)}, u32[]{:S(2)}) copy-start(f32[514,128]{1,0:T(8,128)} %copy-done.14) | copy-start | bytes 789508
  351.7 17.3 %all-to-all-start.12 = ((f32[4,1,128,4]{3,0,1,2:T(4,128)}), f32[4,1,128,4]{3,0,1,2:T(4,128)S(1)}, u32[]{:S(2)}, u32[]{:S(2)}) async-start(f32[4,1,128,4]{3,0,1,2:T(4,128)} %copy.697), calls=%async_computation.12 | async-start | bytes 524288 | tf_op jit(solution)/shard_map/all_to_all | solution.py:73
  356.4 284.2 %all-reduce.50.cloned.1.call-start = ((), (), s32[]{:S(2)}) async-start(), calls=%async_computation.13 | async-start | bytes 262144 | tf_op jit(solution)/shard_map/psum | solution.py:138
  (67 other events, 141.9 us)
Sparse Core Ops, SparseCore 0:
  373.0 267.4 all-reduce.49
where the time goes:
time: 660 us; the launch traced here: 649 us
  waiting for transfers between devices  235 us (36%)
  blocking collectives  215 us (33%)
  local copies, waits for them, and re-layouts  70 us (11%)
  starting transfers between devices  50.5 us (8%)
  matrix products  39.1 us (6%)
  other arithmetic  22.5 us (3%)
  between operations  16.6 us (3%)
    psum x1, waiting for transfers between devices, on_device(): lax.psum((sums[0], sums[1], sums[2], sums[3], sums[4], sums[5]), ('band',...  162 us
    psum x1, blocking collectives, on_device(): lax.psum((sums[0], sums[1], sums[2], sums[3], sums[4], sums[5]), ('band',...  105 us
    all_to_all x3, blocking collectives, to_rows(): lax.all_to_all(field, 'band', split_axis=2, concat_axis=3, tiled=True)  55.7 us
    all_to_all x3, blocking collectives, to_columns(): lax.all_to_all(field, 'band', split_axis=3, concat_axis=2, tiled=True)  54.9 us
    all_to_all x3, waiting for transfers between devices, to_rows(): lax.all_to_all(field, 'band', split_axis=2, concat_axis=3, tiled=True)  35.5 us
    all_to_all x3, waiting for transfers between devices, to_columns(): lax.all_to_all(field, 'band', split_axis=3, concat_axis=2, tiled=True)  34.8 us
    all_to_all x3, starting transfers between devices, to_columns(): lax.all_to_all(field, 'band', split_axis=3, concat_axis=2, tiled=True)  18.9 us
    all_to_all x1, starting transfers between devices, on_device(): lax.all_to_all(stacked, 'band', split_axis=2, concat_axis=1, tiled=True)  17.3 us
  transfers between devices with their start and end apart: 8, of which 8 were waited for; matrix products, arithmetic and copies ran while one was open for 2% of the time, Pallas kernels for 0%

commit v1 on v0

v1 whole, which is shorter than its diff:
```python
import functools
import math

import jax
import jax.numpy as jnp
from jax import lax
from jax.experimental import pallas as pl
from jax.experimental.pallas import tpu as pltpu
from jax.sharding import PartitionSpec as P

STEPS = 3
WIDTH = 128
F32 = jnp.float32
BF16 = jnp.bfloat16
MESH = pl.DeviceIdType.MESH
BASE = (-1.0 / 12.0, 7.0 / 12.0, 7.0 / 12.0, -1.0 / 12.0)

NY = 256
GAP = 64
NZ = 640
SLOT_FACE = (1, 2, 3, 0, 4)
NM = 5 * NY
NET_ROWS = 160
GRAD_ROWS = 2 * NET_ROWS


def split(x):
    hi = x.astype(BF16)
    lo = (x - hi.astype(F32)).astype(BF16)
    return hi, lo


def stack(x):
    return jnp.concatenate(split(x), axis=0)


def dot(a, b):
    return lax.dot_general(a, b, (((1,), (0,)), ((), ())), preferred_element_type=F32)


def dot_nt(a, b):
    return lax.dot_general(a, b, (((1,), (1,)), ((), ())), preferred_element_type=F32)


def low_half(shape):
    return lax.broadcasted_iota(jnp.int32, shape, 0) < 4


def pick(a, b):
    return jnp.where(low_half(a.shape), a, b)


def turn(x):
    return pltpu.roll(x, 4, axis=0)


def lane_roll(x, shift):
    return pltpu.roll(x, shift % x.shape[1], axis=1)


def both_rows(block):
    turned = turn(block)
    return pick(block, turned), pick(turned, block)


def to_line(first, second):
    gap = jnp.zeros((first.shape[0], 2 * GAP), F32)
    return jnp.concatenate([lane_roll(jnp.concatenate([first, gap], 1), GAP), second], 1)


def from_line(line):
    return lane_roll(line[:, : NY + 2 * GAP], -GAP)[:, :NY], line[:, NY + 2 * GAP :]


def kernel(
    bands,
    levs,
    loss_scale,
    conc_ref,
    target_ref,
    zwind_ref,
    mwind_ref,
    sea_ref,
    w1_ref,
    b1_ref,
    w2_ref,
    b2_ref,
    w3_ref,
    b3_ref,
    field_ref,
    gw1_ref,
    gb1_ref,
    gw2_ref,
    gb2_ref,
    gw3_ref,
    gb3_ref,
    w1s,
    w2s,
    w3s,
    w3e,
    w2b,
    w1b,
    b2s,
    b3s,
    zcour,
    mcour,
    halo,
    ghalo,
    winds,
    line,
    gline,
    ax_z,
    ax_m,
    h2_z,
    h2_m,
    s1_z,
    s1_m,
    s2_z,
    s2_m,
    st_z,
    st_m,
    cf_z,
    cf_m,
    d1_z,
    d1_m,
    d2_z,
    d2_m,
    pb_z,
    pb_m,
    acc2,
    acc1,
    acc3,
    accb2,
    accp,
    grads,
    r1,
    s1buf,
    r2,
    r3,
    a4,
    full,
    halo_send,
    halo_recv,
    ghalo_send,
    ghalo_recv,
    wind_send,
    wind_recv,
    red_send,
    red_recv,
):
    side_y = math.isqrt(bands)
    side_z = bands // side_y
    band = lax.axis_index("band")
    lev = lax.axis_index("lev")
    my_y = band // side_z
    my_z = band % side_z

    def y_device(ty):
        return {"band": ty * side_z + my_z, "lev": lev}

    def z_device(tz):
        return {"band": my_y * side_z + tz, "lev": lev}

    def lev_device(tl):
        return {"band": band, "lev": tl}

    def band_device(tb):
        return {"band": tb, "lev": lev}

    winds[...] = jnp.zeros_like(winds)
    halo[...] = jnp.zeros_like(halo)
    ghalo[...] = jnp.zeros_like(ghalo)
    barrier = pltpu.get_barrier_semaphore()
    greeted = 0
    for delta in (1, bands - 1, 2, bands - 2):
        pl.semaphore_signal(
            barrier, inc=1, device_id=band_device((band + delta) % bands), device_id_type=MESH
        )
        greeted += 1
    for d in range(1, levs):
        pl.semaphore_signal(
            barrier, inc=1, device_id=lev_device((lev + d) % levs), device_id_type=MESH
        )
        greeted += 1
    for d in range(1, side_y):
        pl.semaphore_signal(
            barrier, inc=1, device_id=y_device((my_y + d) % side_y), device_id_type=MESH
        )
        greeted += 1
    for d in range(1, side_z):
        pl.semaphore_signal(
            barrier, inc=1, device_id=z_device((my_z + d) % side_z), device_id_type=MESH
        )
        greeted += 1

    def prepare(net):
        w1 = w1_ref[net]
        b1 = b1_ref[net : net + 1, :]
        rows = jnp.concatenate([w1, b1, jnp.zeros((11, WIDTH), F32)], 0)
        hi, lo = split(rows)
        hi, lo = hi.astype(F32), lo.astype(F32)
        w1s[net] = jnp.concatenate([hi, hi, lo, jnp.zeros_like(hi)], 0).T.astype(BF16)
        hi, lo = split(rows[0:16])
        w1b[net, 0:16, 0:128] = hi
        w1b[net, 0:16, 128:256] = hi
        w1b[net, 16:32, 0:128] = lo
        w1b[net, 16:32, 128:256] = lo
        w2 = w2_ref[net]
        for ref, mat in ((w2s, w2.T), (w2b, w2)):
            hi, lo = split(mat)
            ref[net, 0:128, 0:128] = hi
            ref[net, 0:128, 128:256] = hi
            ref[net, 128:256, 0:128] = lo
            ref[net, 128:256, 128:256] = lo
        b2s[net] = jnp.broadcast_to(b2_ref[net : net + 1, :], (WIDTH, WIDTH)).T
        w3 = w3_ref[net]
        w3 = w3 - jnp.mean(w3, 0, keepdims=True)
        group = lax.broadcasted_iota(jnp.int32, (16, WIDTH), 0) // 4
        rep = jnp.zeros((16, WIDTH), F32)
        for j in range(4):
            rep = jnp.where(group == j, w3[j : j + 1, :], rep)
        hi, lo = split(rep)
        w3s[net, 0:16, 0:128] = hi
        w3s[net, 0:16, 128:256] = hi
        w3s[net, 16:32, 0:128] = lo
        w3s[net, 16:32, 128:256] = lo
        hi, lo = hi.astype(F32), lo.astype(F32)
        w3e[net] = jnp.concatenate([hi, hi, lo, jnp.zeros((80, WIDTH), F32)], 0).T.astype(BF16)
        b3 = b3_ref[net : net + 1, :]
        b3 = b3 - jnp.mean(b3, 1, keepdims=True)
        mine = (
            lax.broadcasted_iota(jnp.int32, (16, 4), 0) // 4
            == lax.broadcasted_iota(jnp.int32, (16, 4), 1)
        )
        column = jnp.sum(jnp.where(mine, b3, 0.0), 1, keepdims=True)
        place = lax.broadcasted_iota(jnp.int32, (16, WIDTH), 0) // 4
        base = jnp.where((place == 0) | (place == 3), BASE[0], BASE[1])
        b3s[net] = column + base

    def constant_rows(ref, lo_lane, courant, low, high):
        n = courant.shape[1]
        place = lax.broadcasted_iota(jnp.int32, (16, n), 0)
        rows = jnp.where(place == 0, courant, 0.0)
        rows = jnp.where(place == 1, courant * courant, rows)
        rows = jnp.where(place == 2, low, rows)
        rows = jnp.where(place == 3, high, rows)
        rows = jnp.where(place == 4, 1.0, rows)
        hi, lo = split(rows)
        for s in range(STEPS):
            ref[s, 272:288, lo_lane : lo_lane + n] = hi
            ref[s, 304:320, lo_lane : lo_lane + n] = lo
            ref[s, 336:352, lo_lane : lo_lane + n] = hi

    def forward(net, s, lanes, stencil, courant, ax, h2, s1, s2, st, cf):
        hi, lo = split(stencil)
        ax[s, 256:272, lanes] = hi
        ax[s, 288:304, lanes] = lo
        ax[s, 320:336, lanes] = hi
        st[s, :, lanes] = stencil
        one = jnp.tanh(dot(w1s[net, :, 0:96], ax[s, 256:352, lanes]))
        s1[s, :, lanes] = 1.0 - one * one
        pair = stack(one)
        ax[s, 0:256, lanes] = pair
        out = dot(w2s[net], pair)
        bias = b2s[net]
        n = out.shape[1]
        bias = jnp.concatenate([bias] * (n // WIDTH), 1)
        two = jnp.tanh(out[0:128] + out[128:256] + bias)
        s2[s, :, lanes] = 1.0 - two * two
        pair = stack(two)
        h2[s, :, lanes] = pair
        out = dot(w3s[net], pair)
        coef = out[0:16] + out[16:32] + jnp.concatenate([b3s[net]] * (n // WIDTH), 1)
        cf[s, :, lanes] = coef
        terms = coef * stencil
        half = terms[0:8] + terms[8:16]
        return courant * (half + turn(half))

    def backward(net, s, lanes, dflux, courant, d1, d2, pb, s1, s2, st, cf):
        dq = courant * dflux
        dq = jnp.concatenate([dq, dq], 0)
        weighted = dq * st[s, :, lanes]
        hi, lo = split(weighted)
        pb[0:16, lanes] = hi
        pb[16:32, lanes] = lo
        two = dot(w3e[net, :, 0:48], jnp.concatenate([hi, lo, hi], 0)) * s2[s, :, lanes]
        pair = stack(two)
        d2[:, lanes] = pair
        out = dot(w2b[net], pair)
        one = (out[0:128] + out[128:256]) * s1[s, :, lanes]
        pair = stack(one)
        d1[:, lanes] = pair
        out = dot(w1b[net], pair)
        return out[0:16] + out[16:32] + cf[s, :, lanes] * dq, weighted

    def quads(x, m, n):
        return (x[0:m, 0:n] + x[m : 2 * m, n : 2 * n]) + (x[0:m, n : 2 * n] + x[m : 2 * m, 0:n])

    def weight_grads(net, s, lanes, ax, h2, d1, d2, pb):
        out = dot_nt(ax[s, 0:288, lanes], d2[:, lanes])
        acc2[net] += quads(out, 128, 128)
        accb2[net] += out[256:288, 0:128] + out[256:288, 128:256]
        out = dot_nt(ax[s, 256:320, lanes], d1[:, lanes])
        acc1[net] += quads(out, 32, 128)
        out = dot_nt(pb[:, lanes], h2[s, :, lanes])
        acc3[net] += quads(out, 16, 128)

    def lane_fold(x):
        out = x[:, 0:128]
        for i in range(1, x.shape[1] // 128):
            out = out + x[:, 128 * i : 128 * (i + 1)]
        return out

    zchunks = (slice(0, 256), slice(256, 512), slice(512, 640))

    def zonal_stencil():
        c = line[...]
        return jnp.concatenate(
            [pick(lane_roll(c, 1), c), pick(lane_roll(c, -1), lane_roll(c, -2))], 0
        )

    def zonal(s):
        stencil = zonal_stencil()
        parts = [
            forward(
                0, s, lanes, stencil[:, lanes], zcour[:, lanes], ax_z, h2_z, s1_z, s2_z, st_z, cf_z
            )
            for lanes in zchunks
        ]
        flux = jnp.concatenate(parts, 1)
        new = line[...] - (flux - lane_roll(flux, 1))
        halo[s, 2] = pick(*from_line(new))

    def face_stencil(s, face):
        mid = turn(halo[s, 2])
        if face == 1:
            return jnp.concatenate([halo[s, 1], halo[s, 2]], 0)
        if face == 3:
            return jnp.concatenate([halo[s, 2], halo[s, 3]], 0)
        if face == 2:
            return jnp.concatenate([pick(turn(halo[s, 1]), mid), pick(mid, turn(halo[s, 3]))], 0)
        if face == 0:
            before = turn(halo[s, 1])
            return jnp.concatenate([pick(turn(halo[s, 0]), before), pick(before, mid)], 0)
        after = turn(halo[s, 3])
        return jnp.concatenate([pick(mid, after), pick(after, turn(halo[s, 4]))], 0)

    def merid_faces(s, slots):
        fluxes = []
        for slot in slots:
            lanes = slice(slot * NY, (slot + 1) * NY)
            fluxes.append(
                forward(
                    1,
                    s,
                    lanes,
                    face_stencil(s, SLOT_FACE[slot]),
                    mcour[:, lanes],
                    ax_m,
                    h2_m,
                    s1_m,
                    s2_m,
                    st_m,
                    cf_m,
                )
            )
        return fluxes

    def halo_copy(buf, s, which, send, recv):
        delta, slot = ((1, 1), (-1, 3), (2, 0), (-2, 4))[which]
        return pltpu.make_async_remote_copy(
            src_ref=buf.at[s, 2],
            dst_ref=buf.at[s, slot],
            send_sem=send.at[s, which],
            recv_sem=recv.at[s, which],
            device_id=band_device(band + delta),
            device_id_type=MESH,
        )

    has_target = (band < bands - 1, band >= 1, band < bands - 2, band >= 2)
    has_source = (band >= 1, band < bands - 1, band >= 2, band < bands - 2)

    def halo_start(buf, s, send, recv, which_all):
        for which in which_all:

            @pl.when(has_target[which])
            def _():
                halo_copy(buf, s, which, send, recv).start()

    def halo_wait(buf, s, send, recv, which_all):
        for which in which_all:

            @pl.when(has_source[which])
            def _():
                halo_copy(buf, s, which, send, recv).wait_recv()

    def halo_drain(buf, s, send, recv, which_all):
        for which in which_all:

            @pl.when(has_target[which])
            def _():
                halo_copy(buf, s, which, send, recv).wait_send()

    prepare(0)
    rows = [conc_ref[b, 0, r : r + 1, :] for r in range(2) for b in range(4)]
    line[...] = to_line(*both_rows(jnp.concatenate(rows, 0)))
    sea = sea_ref[...].astype(F32)
    zw = to_line(zwind_ref[0, 0:1, :], zwind_ref[0, 1:2, :])
    zs = to_line(sea[0:1, :], sea[1:2, :])
    courant = 0.5 * (zw + lane_roll(zw, -1))
    zcour[...] = jnp.broadcast_to(courant, (8, NZ))
    constant_rows(ax_z, 0, courant, zs, lane_roll(zs, -1))
    winds[0, 2, 0:2, :] = mwind_ref[0]
    winds[0, 2, 2:4, :] = sea
    for acc in (acc2, acc1, acc3, accb2, accp):
        acc[...] = jnp.zeros_like(acc)

    def forward_step(s, carry):
        zonal(s)

        @pl.when(s == 0)
        def _():
            pl.semaphore_wait(barrier, greeted)
            halo_start(winds, 0, wind_send, wind_recv, (0, 1))

        halo_start(halo, s, halo_send, halo_recv, (0, 1, 2, 3))

        @pl.when(s == 0)
        def _():
            prepare(1)
            halo_wait(winds, 0, wind_send, wind_recv, (0, 1))
            w = [winds[0, 1 + i // 2, i % 2 : i % 2 + 1, :] for i in range(6)]
            m = [winds[0, 1 + i // 2, 2 + i % 2 : 3 + i % 2, :] for i in range(6)]
            for slot, face in enumerate(SLOT_FACE):
                courant = 0.5 * (w[face] + w[face + 1])
                mcour[:, slot * NY : (slot + 1) * NY] = jnp.broadcast_to(courant, (8, NY))
                constant_rows(ax_m, slot * NY, courant, m[face], m[face + 1])

        @pl.when(s > 0)
        def _():
            halo_wait(halo, s - 1, halo_send, halo_recv, (2, 3))
            merid_faces(s - 1, (3, 4))

        halo_wait(halo, s, halo_send, halo_recv, (0, 1))
        f1, f2, f3 = merid_faces(s, (0, 1, 2))
        new = halo[s, 2] - pick(f2 - f1, f3 - f2)
        line[...] = to_line(*both_rows(new))

        @pl.when(s == STEPS - 1)
        def _():
            rows = [target_ref[b, 0, r : r + 1, :] for r in range(2) for b in range(4)]
            ghalo[STEPS - 1, 2] = (new - jnp.concatenate(rows, 0)) * loss_scale
            halo_start(ghalo, STEPS - 1, ghalo_send, ghalo_recv, (0, 1))
            for r in range(2):
                for b in range(4):
                    field_ref[b, 0, r : r + 1, :] = new[4 * r + b : 4 * r + b + 1, :]

        return carry

    lax.fori_loop(0, STEPS, forward_step, 0)
    halo_wait(halo, STEPS - 1, halo_send, halo_recv, (2, 3))
    merid_faces(STEPS - 1, (3, 4))

    def backward_step(i, carry):
        s = STEPS - 1 - i
        halo_wait(ghalo, s, ghalo_send, ghalo_recv, (0, 1))
        g = []
        for block in (1, 2, 3):
            g.extend(both_rows(ghalo[s, block]))
        lows, highs = [None] * 5, [None] * 5
        first = None
        inner = None
        for slot, face in enumerate(SLOT_FACE):
            lanes = slice(slot * NY, (slot + 1) * NY)
            out, weighted = backward(
                1,
                s,
                lanes,
                g[face + 1] - g[face],
                mcour[:, lanes],
                d1_m,
                d2_m,
                pb_m,
                s1_m,
                s2_m,
                st_m,
                cf_m,
            )
            lows[face], highs[face] = out[0:8], out[8:16]
            if slot == 0:
                first = lane_fold(weighted)
            elif slot == 1:
                inner = lane_fold(weighted)
            elif slot == 2:
                inner = inner + lane_fold(weighted)
        new = ghalo[s, 2] + (highs[1] + lows[3])
        new = new + turn(pick(highs[2] + lows[4], highs[0] + lows[2]))
        accp[1] += inner

        @pl.when(band == 0)
        def _():
            accp[1] += first

        gline[...] = to_line(*both_rows(new))
        gz = gline[...]
        dflux = lane_roll(gz, -1) - gz
        outs = [
            backward(
                0,
                s,
                lanes,
                dflux[:, lanes],
                zcour[:, lanes],
                d1_z,
                d2_z,
                pb_z,
                s1_z,
                s2_z,
                st_z,
                cf_z,
            )
            for lanes in zchunks
        ]
        out = jnp.concatenate([o[0] for o in outs], 1)
        low, high = out[0:8], out[8:16]
        t = pick(lane_roll(low, -1), low) + pick(lane_roll(high, 1), lane_roll(high, 2))
        new = gz + t + turn(t)

        @pl.when(s > 0)
        def _():
            ghalo[jnp.maximum(s - 1, 0), 2] = pick(*from_line(new))
            halo_start(ghalo, s - 1, ghalo_send, ghalo_recv, (0, 1))

        accp[0] += sum(lane_fold(o[1]) for o in outs)
        weight_grads(1, s, slice(NY, 3 * NY), ax_m, h2_m, d1_m, d2_m, pb_m)

        @pl.when(band == 0)
        def _():
            weight_grads(1, s, slice(0, NY), ax_m, h2_m, d1_m, d2_m, pb_m)

        weight_grads(0, s, slice(0, NZ), ax_z, h2_z, d1_z, d2_z, pb_z)
        return carry

    lax.fori_loop(0, STEPS, backward_step, 0)

    centre = jnp.where(
        lax.broadcasted_iota(jnp.int32, (16, 16), 1) // 4
        == lax.broadcasted_iota(jnp.int32, (16, 16), 0),
        0.75,
        -0.25,
    )
    centre = jnp.concatenate([centre, centre], 1).astype(BF16)
    for net in range(2):
        top = net * NET_ROWS
        grads[top : top + 128] = acc2[net]
        grads[top + 128 : top + 160] = acc1[net]
        grads[top + 149 : top + 150] = accb2[net, 20:21, :]
        grads[top + 152 : top + 156] = dot(centre, stack(acc3[net]))[0:4]
        sums = jnp.sum(accp[net], 1, keepdims=True)
        mine = (
            lax.broadcasted_iota(jnp.int32, (16, WIDTH), 0) // 4
            == lax.broadcasted_iota(jnp.int32, (16, WIDTH), 1)
        )
        row = jnp.sum(jnp.where(mine, sums, 0.0), 0, keepdims=True)
        grads[top + 156 : top + 157] = row - jnp.sum(row, 1, keepdims=True) * 0.25

    piece = GRAD_ROWS // levs
    part = piece // side_y
    started = []

    def send(src, dst, index, device):
        copy = pltpu.make_async_remote_copy(
            src_ref=src,
            dst_ref=dst,
            send_sem=red_send.at[index],
            recv_sem=red_recv.at[index],
            device_id=device,
            device_id_type=MESH,
        )
        copy.start()
        started.append(copy)
        return copy

    def wait(copies):
        for copy in copies:
            copy.wait_recv()

    at = 0
    copies = []
    for d in range(1, levs):
        tl = (lev + d) % levs
        src = grads.at[pl.ds(pl.multiple_of(tl * piece, 8), piece)]
        copies.append(send(src, r1.at[d - 1], at, lev_device(tl)))
        at += 1
    total = grads[pl.ds(pl.multiple_of(lev * piece, 8), piece)]
    wait(copies)
    for d in range(1, levs):
        total = total + r1[d - 1]
    for i in range(side_y):
        s1buf[i] = total[i * part : (i + 1) * part]
    copies = []
    for d in range(1, side_y):
        ty = (my_y + d) % side_y
        copies.append(send(s1buf.at[ty], r2.at[d - 1], at, y_device(ty)))
        at += 1
    total = s1buf[my_y]
    wait(copies)
    for d in range(1, side_y):
        total = total + r2[d - 1]
    r3[my_z] = total
    copies = []
    for d in range(1, side_z):
        tz = (my_z + d) % side_z
        copies.append(send(r3.at[my_z], r3.at[my_z], at, z_device(tz)))
        at += 1
    wait(copies)
    total = r3[0]
    for i in range(1, side_z):
        total = total + r3[i]
    a4[my_y] = total
    copies = []
    for d in range(1, side_y):
        ty = (my_y + d) % side_y
        copies.append(send(a4.at[my_y], a4.at[my_y], at, y_device(ty)))
        at += 1
    wait(copies)
    for i in range(side_y):
        full[lev, i * part : (i + 1) * part] = a4[i]
    copies = []
    for d in range(1, levs):
        tl = (lev + d) % levs
        copies.append(send(full.at[lev], full.at[lev], at, lev_device(tl)))
        at += 1
    wait(copies)
    everything = full[...].reshape(GRAD_ROWS, WIDTH)
    for net in range(2):
        top = net * NET_ROWS
        gw2_ref[net] = everything[top : top + 128]
        gw1_ref[net] = everything[top + 128 : top + 148]
        gb1_ref[net : net + 1] = everything[top + 148 : top + 149]
        gb2_ref[net : net + 1] = everything[top + 149 : top + 150]
        gw3_ref[net] = everything[top + 152 : top + 156]
        gb3_ref[net : net + 1] = everything[top + 156 : top + 157, 0:4]

    for copy in started:
        copy.wait_send()
    halo_drain(winds, 0, wind_send, wind_recv, (0, 1))
    for s in range(STEPS):
        halo_drain(halo, s, halo_send, halo_recv, (0, 1, 2, 3))
        halo_drain(ghalo, s, ghalo_send, ghalo_recv, (0, 1))


def on_device(bands, levs, loss_scale, *args):
    piece = GRAD_ROWS // levs
    side_y = math.isqrt(bands)
    side_z = bands // side_y
    part = piece // side_y
    reductions = 2 * (levs - 1) + 2 * (side_y - 1) + (side_z - 1)
    vmem = pltpu.VMEM
    sweeps = [NZ, NM]
    scratch = [
        vmem((2, 128, 128), BF16),
        vmem((2, 256, 256), BF16),
        vmem((2, 32, 256), BF16),
        vmem((2, 128, 128), BF16),
        vmem((2, 256, 256), BF16),
        vmem((2, 32, 256), BF16),
        vmem((2, 128, 128), F32),
        vmem((2, 16, 128), F32),
        vmem((8, NZ), F32),
        vmem((8, NM), F32),
        vmem((STEPS, 5, 8, NY), F32),
        vmem((STEPS, 5, 8, NY), F32),
        vmem((1, 5, 8, NY), F32),
        vmem((8, NZ), F32),
        vmem((8, NZ), F32),
        *[vmem((STEPS, 352, n), BF16) for n in sweeps],
        *[vmem((STEPS, 256, n), BF16) for n in sweeps],
        *[vmem((STEPS, 128, n), F32) for n in sweeps],
        *[vmem((STEPS, 128, n), F32) for n in sweeps],
        *[vmem((STEPS, 16, n), F32) for n in sweeps],
        *[vmem((STEPS, 16, n), F32) for n in sweeps],
        *[vmem((256, n), BF16) for n in sweeps],
        *[vmem((256, n), BF16) for n in sweeps],
        *[vmem((32, n), BF16) for n in sweeps],
        vmem((2, 128, 128), F32),
        vmem((2, 32, 128), F32),
        vmem((2, 16, 128), F32),
        vmem((2, 32, 128), F32),
        vmem((2, 16, 128), F32),
        vmem((GRAD_ROWS, 128), F32),
        vmem((levs - 1, piece, 128), F32),
        vmem((side_y, part, 128), F32),
        vmem((side_y - 1, part, 128), F32),
        vmem((side_z, part, 128), F32),
        vmem((side_y, part, 128), F32),
        vmem((levs, piece, 128), F32),
        pltpu.SemaphoreType.DMA((STEPS, 4)),
        pltpu.SemaphoreType.DMA((STEPS, 4)),
        pltpu.SemaphoreType.DMA((STEPS, 4)),
        pltpu.SemaphoreType.DMA((STEPS, 4)),
        pltpu.SemaphoreType.DMA((1, 4)),
        pltpu.SemaphoreType.DMA((1, 4)),
        pltpu.SemaphoreType.DMA((reductions,)),
        pltpu.SemaphoreType.DMA((reductions,)),
    ]
    out_shape = [jax.ShapeDtypeStruct(args[0].shape, F32)] + [
        jax.ShapeDtypeStruct(args[i].shape, F32) for i in range(5, 11)
    ]
    return tuple(
        pl.pallas_call(
            functools.partial(kernel, bands, levs, loss_scale),
            out_shape=out_shape,
            in_specs=[pl.BlockSpec(memory_space=pltpu.VMEM)] * 11,
            out_specs=[pl.BlockSpec(memory_space=pltpu.VMEM)] * 7,
            scratch_shapes=scratch,
            compiler_params=pltpu.CompilerParams(
                collective_id=0, has_side_effects=True, vmem_limit_bytes=48 * 1024 * 1024
            ),
            name="advection_step",
        )(*args)
    )


def solution(mesh):
    bands, levs = mesh.shape["band"], mesh.shape["lev"]
    loss_scale = 1.0 / math.sqrt(4 * levs * 2 * bands * NY)
    return jax.shard_map(
        functools.partial(on_device, bands, levs, loss_scale),
        mesh=mesh,
        in_specs=(
            P(None, "lev", "band", None),
            P(None, "lev", "band", None),
            P("lev", "band", None),
            P("lev", "band", None),
            P("band", None),
            P(),
            P(),
            P(),
            P(),
            P(),
            P(),
        ),
        out_specs=(P(None, "lev", "band", None), P(), P(), P(), P(), P(), P()),
        check_vma=False,
    )
```

time: 660 us -> 85.9 us (0.13); the launches traced: 649 us -> 85.7 us
  waiting for transfers between devices: 235 us -> 0 us
  blocking collectives: 215 us -> 0 us
  Pallas kernels: 0 us -> 79.1 us
  local copies, waits for them, and re-layouts: 70 us -> 5.87 us
  starting transfers between devices: 50.5 us -> 0 us
  matrix products: 39.1 us -> 0 us
  other arithmetic: 22.5 us -> 0 us
  between operations: 16.6 us -> 0.78 us
    psum x1 -> x0, waiting for transfers between devices: 162 us -> none  [on_device(): lax.psum((sums[0], sums[1], sums[2], sums[3], sums[4], sums[5]), ('band',...]
    all_to_all x6 -> x0, blocking collectives: 111 us -> none  [the longest x3 55.7 us: to_rows(): lax.all_to_all(field, 'band', split_axis=2, concat_axis=3, tiled=True)]
    psum x1 -> x0, blocking collectives: 105 us -> none  [on_device(): lax.psum((sums[0], sums[1], sums[2], sums[3], sums[4], sums[5]), ('band',...]
    pallas_call x0 -> x1, Pallas kernels: none -> 79.1 us  [on_device(): pl.pallas_call(functools.partial(kernel, bands, levs, loss_scale), out_sh...]
    all_to_all x7 -> x0, waiting for transfers between devices: 73.4 us -> none  [the longest x3 35.5 us: to_rows(): lax.all_to_all(field, 'band', split_axis=2, concat_axis=3, tiled=True)]
    all_to_all x7 -> x0, starting transfers between devices: 50.4 us -> none  [the longest x3 18.9 us: to_columns(): lax.all_to_all(field, 'band', split_axis=3, concat_axis=2, tiled=True)]
    dot_general x53 -> x0, matrix products: 39.1 us -> none  [the longest x18 15.9 us: face_flux(): jnp.dot(w_second.T, hidden_one, precision=lax.Precision.HIGHEST)]
    all_to_all x31 -> x0, local copies, waits for them, and re-layouts: 18.6 us -> none  [the longest x18 14.1 us: to_columns(): lax.all_to_all(field, 'band', split_axis=3, concat_axis=2, tiled=True)]
  transfers between devices with their start and end apart: 8 -> 0, of which waited for: 8 -> 0; matrix products, arithmetic and copies ran while one was open for 2% -> 0% of each run, Pallas kernels for 0% -> 0%
where the time goes in v1:
time: 85.9 us; the launch traced here: 85.7 us
  Pallas kernels  79.1 us (92%)
  local copies, waits for them, and re-layouts  5.87 us (7%)
    pallas_call x1, Pallas kernels, on_device(): pl.pallas_call(functools.partial(kernel, bands, levs, loss_scale), out_sh...  79.1 us
    unnamed x27, local copies, waits for them, and re-layouts  5.25 us

profile of v1, /device:TPU:1, one launch (start us, length us, event | category | flops | bytes accessed | tf_op | source)
XLA Modules:
  0.0 85.7 jit_solution(5639457079492897087)
XLA Ops:
  0.6 0.0 copy-start.9
  0.6 0.0 copy-start.3
  0.7 0.0 copy-start.8
  0.7 0.0 copy-start.7
  0.7 0.0 copy-start.6
  0.7 0.0 copy-start.5
  0.7 0.0 copy-start.4
  0.7 0.0 copy-start.2
  0.7 0.0 copy-start.1
  0.7 0.8 copy.18.w1_ref
  1.5 0.0 copy-done.9
  1.5 0.0 copy-done.3
  1.5 0.0 copy-done.8
  1.5 0.0 copy-done.7
  1.5 0.0 copy-done.6
  1.5 0.0 copy-done.5
  1.5 0.0 copy-done.4
  1.6 0.0 copy-done.2
  1.6 0.0 copy-done.1
  1.6 0.0 copy-start
  1.6 0.9 %copy-done = f32[2,128,128]{2,1,0:T(8,128)S(1)} copy-done((f32[2,128,128]{2,1,0:T(8,128)S(1)}, f32[2,128,128]{2,1,0:T(8,128)}, u32[]{:S(2)}) %copy-start) | copy-done | bytes 131096
  2.5 79.1 %advection_step.1 = (f32[4,1,2,256]{3,2,1,0:T(2,128)S(1)}, f32[2,20,128]{2,1,0:T(8,128)S(1)}, f32[2,128]{1,0:T(2,128)S(1)}, f32[2,128,128]{2,1,0:T(8,128)S(1)}, ...) custom-call(f32[4,1,2,256]{3,2,1,0:T(2,128)S(1)} %copy-done.1, f32[4,1,2,256]{3,2,1,0:T(2,128)S(1)} %copy-done.2, ...), custom_call_target="tpu_custom_call" | custom-call | tf_op jit(solution)/shard_map/advection_step/pallas_call | solution.py:711
  81.6 0.6 copy.19
  82.2 0.6 copy.26
  82.8 0.6 copy.27
  83.3 0.7 copy.28
  84.0 0.6 copy.29
  84.6 0.6 copy.30
  85.2 0.6 copy.31
Async XLA Ops:
  0.6 0.9 %copy-start.9 = (f32[2,4]{1,0:T(2,128)S(1)}, f32[2,4]{1,0:T(2,128)}, u32[]{:S(2)}) copy-start(f32[2,4]{1,0:T(2,128)} %b3_ref.1) | copy-start | bytes 100
  0.6 0.9 %copy-start.3 = (f32[2,4,128]{2,1,0:T(4,128)S(1)}, f32[2,4,128]{2,1,0:T(4,128)}, u32[]{:S(2)}) copy-start(f32[2,4,128]{2,1,0:T(4,128)} %w3_ref.1) | copy-start | bytes 12292
  0.7 0.9 %copy-start.8 = (f32[2,128]{1,0:T(2,128)S(1)}, f32[2,128]{1,0:T(2,128)}, u32[]{:S(2)}) copy-start(f32[2,128]{1,0:T(2,128)} %b2_ref.1) | copy-start | bytes 3076
  0.7 0.9 copy-start.7
  0.7 0.9 copy-start.6
  0.7 0.9 copy-start.5
  0.7 0.9 copy-start.4
  0.7 0.9 copy-start.2
  0.7 0.9 copy-start.1
  1.6 0.9 %copy-start = (f32[2,128,128]{2,1,0:T(8,128)S(1)}, f32[2,128,128]{2,1,0:T(8,128)}, u32[]{:S(2)}) copy-start(f32[2,128,128]{2,1,0:T(8,128)} %w2_ref.1) | copy-start | bytes 393220

commit v2 on v1

--- a/solution.py
+++ b/solution.py
@@ -42,6 +42,22 @@
     return lax.dot_general(a, b, (((1,), (1,)), ((), ())), preferred_element_type=F32)
 
 
+def run(parts, skew=0):
+    results = [None] * len(parts)
+    live = set(range(len(parts)))
+    tick = 0
+    while live:
+        for i in sorted(live):
+            if tick >= i * skew:
+                try:
+                    next(parts[i])
+                except StopIteration as stop:
+                    results[i] = stop.value
+                    live.discard(i)
+        tick += 1
+    return results
+
+
 def low_half(shape):
     return lax.broadcasted_iota(jnp.int32, shape, 0) < 4
 
@@ -76,6 +92,24 @@
     bands,
     levs,
     loss_scale,
+    conc_hbm,
+    target_hbm,
+    zwind_hbm,
+    mwind_hbm,
+    sea_hbm,
+    w1_hbm,
+    b1_hbm,
+    w2_hbm,
+    b2_hbm,
+    w3_hbm,
+    b3_hbm,
+    field_ref,
+    gw1_ref,
+    gb1_ref,
+    gw2_ref,
+    gb2_ref,
+    gw3_ref,
+    gb3_ref,
     conc_ref,
     target_ref,
     zwind_ref,
@@ -87,13 +121,7 @@
     b2_ref,
     w3_ref,
     b3_ref,
-    field_ref,
-    gw1_ref,
-    gb1_ref,
-    gw2_ref,
-    gb2_ref,
-    gw3_ref,
-    gb3_ref,
+    input_sem,
     w1s,
     w2s,
     w3s,
@@ -147,6 +175,8 @@
     wind_recv,
     red_send,
     red_recv,
+    first_send,
+    first_recv,
 ):
     side_y = math.isqrt(bands)
     side_z = bands // side_y
@@ -166,6 +196,27 @@
 
     def band_device(tb):
         return {"band": tb, "lev": lev}
+
+    inputs = [
+        pltpu.make_async_copy(src, dst, input_sem.at[i])
+        for i, (src, dst) in enumerate(
+            (
+                (w2_hbm, w2_ref),
+                (w1_hbm, w1_ref),
+                (b1_hbm, b1_ref),
+                (b2_hbm, b2_ref),
+                (w3_hbm, w3_ref),
+                (b3_hbm, b3_ref),
+                (conc_hbm, conc_ref),
+                (zwind_hbm, zwind_ref),
+                (sea_hbm, sea_ref),
+                (mwind_hbm, mwind_ref),
+                (target_hbm, target_ref),
+            )
+        )
+    ]
+    for copy in inputs:
+        copy.start()
 
     winds[...] = jnp.zeros_like(winds)
     halo[...] = jnp.zeros_like(halo)
@@ -194,7 +245,7 @@
         greeted += 1
 
     def prepare(net):
-        w1 = w1_ref[net]
+        w1 = w1_ref[:, net, :]
         b1 = b1_ref[net : net + 1, :]
         rows = jnp.concatenate([w1, b1, jnp.zeros((11, WIDTH), F32)], 0)
         hi, lo = split(rows)
@@ -257,11 +308,15 @@
         ax[s, 288:304, lanes] = lo
         ax[s, 320:336, lanes] = hi
         st[s, :, lanes] = stencil
-        one = jnp.tanh(dot(w1s[net, :, 0:96], ax[s, 256:352, lanes]))
+        one = dot(w1s[net, :, 0:96], ax[s, 256:352, lanes])
+        yield
+        one = jnp.tanh(one)
         s1[s, :, lanes] = 1.0 - one * one
         pair = stack(one)
         ax[s, 0:256, lanes] = pair
+        yield
         out = dot(w2s[net], pair)
+        yield
         bias = b2s[net]
         n = out.shape[1]
         bias = jnp.concatenate([bias] * (n // WIDTH), 1)
@@ -269,7 +324,9 @@
         s2[s, :, lanes] = 1.0 - two * two
         pair = stack(two)
         h2[s, :, lanes] = pair
+        yield
         out = dot(w3s[net], pair)
+        yield
         coef = out[0:16] + out[16:32] + jnp.concatenate([b3s[net]] * (n // WIDTH), 1)
         cf[s, :, lanes] = coef
         terms = coef * stencil
@@ -283,14 +340,21 @@
         hi, lo = split(weighted)
         pb[0:16, lanes] = hi
         pb[16:32, lanes] = lo
-        two = dot(w3e[net, :, 0:48], jnp.concatenate([hi, lo, hi], 0)) * s2[s, :, lanes]
+        yield
+        two = dot(w3e[net, :, 0:48], jnp.concatenate([hi, lo, hi], 0))
+        yield
+        two = two * s2[s, :, lanes]
         pair = stack(two)
         d2[:, lanes] = pair
+        yield
         out = dot(w2b[net], pair)
+        yield
         one = (out[0:128] + out[128:256]) * s1[s, :, lanes]
         pair = stack(one)
         d1[:, lanes] = pair
+        yield
         out = dot(w1b[net], pair)
+        yield
         return out[0:16] + out[16:32] + cf[s, :, lanes] * dq, weighted
 
     def quads(x, m, n):
@@ -321,12 +385,14 @@
 
     def zonal(s):
         stencil = zonal_stencil()
-        parts = [
-            forward(
-                0, s, lanes, stencil[:, lanes], zcour[:, lanes], ax_z, h2_z, s1_z, s2_z, st_z, cf_z
-            )
-            for lanes in zchunks
-        ]
+        parts = run(
+            [
+                forward(
+                    0, s, lanes, stencil[:, lanes], zcour[:, lanes], ax_z, h2_z, s1_z, s2_z, st_z, cf_z
+                )
+                for lanes in zchunks
+            ]
+        )
         flux = jnp.concatenate(parts, 1)
         new = line[...] - (flux - lane_roll(flux, 1))
         halo[s, 2] = pick(*from_line(new))
@@ -364,7 +430,7 @@
                     cf_m,
                 )
             )
-        return fluxes
+        return run(fluxes)
 
     def halo_copy(buf, s, which, send, recv):
         delta, slot = ((1, 1), (-1, 3), (2, 0), (-2, 4))[which]
@@ -401,6 +467,8 @@
             def _():
                 halo_copy(buf, s, which, send, recv).wait_send()
 
+    for copy in inputs:
+        copy.wait()
     prepare(0)
     rows = [conc_ref[b, 0, r : r + 1, :] for r in range(2) for b in range(4)]
     line[...] = to_line(*both_rows(jnp.concatenate(rows, 0)))
@@ -461,8 +529,7 @@
     halo_wait(halo, STEPS - 1, halo_send, halo_recv, (2, 3))
     merid_faces(STEPS - 1, (3, 4))
 
-    def backward_step(i, carry):
-        s = STEPS - 1 - i
+    def merid_back(s):
         halo_wait(ghalo, s, ghalo_send, ghalo_recv, (0, 1))
         g = []
         for block in (1, 2, 3):
@@ -470,9 +537,10 @@
         lows, highs = [None] * 5, [None] * 5
         first = None
         inner = None
+        parts = []
         for slot, face in enumerate(SLOT_FACE):
             lanes = slice(slot * NY, (slot + 1) * NY)
-            out, weighted = backward(
+            part = backward(
                 1,
                 s,
                 lanes,
@@ -486,6 +554,9 @@
                 st_m,
                 cf_m,
             )
+            parts.append(part)
+        for slot, (out, weighted) in enumerate(run(parts)):
+            face = SLOT_FACE[slot]
             lows[face], highs[face] = out[0:8], out[8:16]
             if slot == 0:
                 first = lane_fold(weighted)
@@ -502,46 +573,57 @@
             accp[1] += first
 
         gline[...] = to_line(*both_rows(new))
+
+    def zonal_back(s):
         gz = gline[...]
         dflux = lane_roll(gz, -1) - gz
-        outs = [
-            backward(
-                0,
-                s,
-                lanes,
-                dflux[:, lanes],
-                zcour[:, lanes],
-                d1_z,
-                d2_z,
-                pb_z,
-                s1_z,
-                s2_z,
-                st_z,
-                cf_z,
-            )
-            for lanes in zchunks
-        ]
+        outs = run(
+            [
+                backward(
+                    0,
+                    s,
+                    lanes,
+                    dflux[:, lanes],
+                    zcour[:, lanes],
+                    d1_z,
+                    d2_z,
+                    pb_z,
+                    s1_z,
+                    s2_z,
+                    st_z,
+                    cf_z,
+                )
+                for lanes in zchunks
+            ]
+        )
         out = jnp.concatenate([o[0] for o in outs], 1)
         low, high = out[0:8], out[8:16]
         t = pick(lane_roll(low, -1), low) + pick(lane_roll(high, 1), lane_roll(high, 2))
         new = gz + t + turn(t)
 
-        @pl.when(s > 0)
-        def _():
-            ghalo[jnp.maximum(s - 1, 0), 2] = pick(*from_line(new))
-            halo_start(ghalo, s - 1, ghalo_send, ghalo_recv, (0, 1))
-
         accp[0] += sum(lane_fold(o[1]) for o in outs)
+        return pick(*from_line(new))
+
+    def merid_weights(s):
         weight_grads(1, s, slice(NY, 3 * NY), ax_m, h2_m, d1_m, d2_m, pb_m)
 
         @pl.when(band == 0)
         def _():
             weight_grads(1, s, slice(0, NY), ax_m, h2_m, d1_m, d2_m, pb_m)
 
+    def zonal_weights(s):
         weight_grads(0, s, slice(0, NZ), ax_z, h2_z, d1_z, d2_z, pb_z)
+
+    def backward_step(i, carry):
+        s = STEPS - 1 - i
+        merid_back(s)
+        ghalo[s - 1, 2] = zonal_back(s)
+        halo_start(ghalo, s - 1, ghalo_send, ghalo_recv, (0, 1))
+        merid_weights(s)
+        zonal_weights(s)
         return carry
 
-    lax.fori_loop(0, STEPS, backward_step, 0)
+    lax.fori_loop(0, STEPS - 1, backward_step, 0)
 
     centre = jnp.where(
         lax.broadcasted_iota(jnp.int32, (16, 16), 1) // 4
@@ -550,7 +632,8 @@
         -0.25,
     )
     centre = jnp.concatenate([centre, centre], 1).astype(BF16)
-    for net in range(2):
+
+    def gather_net(net):
         top = net * NET_ROWS
         grads[top : top + 128] = acc2[net]
         grads[top + 128 : top + 160] = acc1[net]
@@ -585,17 +668,57 @@
         for copy in copies:
             copy.wait_recv()
 
+    wide = levs // 2
+    core = lev % 2
+    my_x = lev // 2
+
+    def first_copy(net, k):
+        tx = (my_x + k) % wide
+        slot = 2 * k + core
+        row = pl.multiple_of(net * NET_ROWS + tx * piece, 8)
+        return pltpu.make_async_remote_copy(
+            src_ref=grads.at[pl.ds(row, piece)],
+            dst_ref=r1.at[slot],
+            send_sem=first_send.at[net, k],
+            recv_sem=first_recv.at[slot],
+            device_id=lev_device(2 * tx + net),
+            device_id_type=MESH,
+        )
+
+    def send_net(net):
+        for k in range(wide - 1, 0, -1):
+            first_copy(net, k).start()
+
+        @pl.when(core != net)
+        def _():
+            first_copy(net, 0).start()
+
+    def drain_net(net):
+        for k in range(1, wide):
+            first_copy(net, k).wait_send()
+
+        @pl.when(core != net)
+        def _():
+            first_copy(net, 0).wait_send()
+
+    def arrived(slot):
+        pltpu.make_async_copy(r1.at[slot], r1.at[slot], first_recv.at[slot]).wait()
+        return r1[slot]
+
+    merid_back(0)
+    merid_weights(0)
+    gather_net(1)
+    send_net(1)
+    zonal_back(0)
+    zonal_weights(0)
+    gather_net(0)
+    send_net(0)
+    row = pl.multiple_of(core * NET_ROWS + my_x * piece, 8)
+    total = grads[pl.ds(row, piece)] + arrived(1 - core)
+    for k in range(1, wide):
+        for c in range(2):
+            total = total + arrived(2 * k + c)
     at = 0
-    copies = []
-    for d in range(1, levs):
-        tl = (lev + d) % levs
-        src = grads.at[pl.ds(pl.multiple_of(tl * piece, 8), piece)]
-        copies.append(send(src, r1.at[d - 1], at, lev_device(tl)))
-        at += 1
-    total = grads[pl.ds(pl.multiple_of(lev * piece, 8), piece)]
-    wait(copies)
-    for d in range(1, levs):
-        total = total + r1[d - 1]
     for i in range(side_y):
         s1buf[i] = total[i * part : (i + 1) * part]
     copies = []
@@ -632,11 +755,11 @@
         copies.append(send(full.at[lev], full.at[lev], at, lev_device(tl)))
         at += 1
     wait(copies)
-    everything = full[...].reshape(GRAD_ROWS, WIDTH)
     for net in range(2):
-        top = net * NET_ROWS
+        everything = jnp.concatenate([full[2 * x + net] for x in range(wide)], 0)
+        top = 0
         gw2_ref[net] = everything[top : top + 128]
-        gw1_ref[net] = everything[top + 128 : top + 148]
+        gw1_ref[:, net, :] = everything[top + 128 : top + 148]
         gb1_ref[net : net + 1] = everything[top + 148 : top + 149]
         gb2_ref[net : net + 1] = everything[top + 149 : top + 150]
         gw3_ref[net] = everything[top + 152 : top + 156]
@@ -644,6 +767,8 @@
 
     for copy in started:
         copy.wait_send()
+    drain_net(0)
+    drain_net(1)
     halo_drain(winds, 0, wind_send, wind_recv, (0, 1))
     for s in range(STEPS):
         halo_drain(halo, s, halo_send, halo_recv, (0, 1, 2, 3))
@@ -655,10 +780,14 @@
     side_y = math.isqrt(bands)
     side_z = bands // side_y
     part = piece // side_y
-    reductions = 2 * (levs - 1) + 2 * (side_y - 1) + (side_z - 1)
+    reductions = (levs - 1) + 2 * (side_y - 1) + (side_z - 1)
     vmem = pltpu.VMEM
     sweeps = [NZ, NM]
+    args = list(args)
+    args[5] = jnp.transpose(args[5], (1, 0, 2))
     scratch = [
+        *[vmem(arg.shape, arg.dtype) for arg in args],
+        pltpu.SemaphoreType.DMA((len(args),)),
         vmem((2, 128, 128), BF16),
         vmem((2, 256, 256), BF16),
         vmem((2, 32, 256), BF16),
@@ -689,7 +818,7 @@
         vmem((2, 32, 128), F32),
         vmem((2, 16, 128), F32),
         vmem((GRAD_ROWS, 128), F32),
-        vmem((levs - 1, piece, 128), F32),
+        vmem((levs, piece, 128), F32),
         vmem((side_y, part, 128), F32),
         vmem((side_y - 1, part, 128), F32),
         vmem((side_z, part, 128), F32),
@@ -703,23 +832,45 @@
         pltpu.SemaphoreType.DMA((1, 4)),
         pltpu.SemaphoreType.DMA((reductions,)),
         pltpu.SemaphoreType.DMA((reductions,)),
+        pltpu.SemaphoreType.DMA((2, levs // 2)),
+        pltpu.SemaphoreType.DMA((levs,)),
     ]
     out_shape = [jax.ShapeDtypeStruct(args[0].shape, F32)] + [
         jax.ShapeDtypeStruct(args[i].shape, F32) for i in range(5, 11)
     ]
-    return tuple(
+    results = pl.pallas_call(
+        functools.partial(kernel, bands, levs, loss_scale),
+        out_shape=out_shape,
+        in_specs=[pl.BlockSpec(memory_space=pltpu.HBM)] * 11,
+        out_specs=[pl.BlockSpec(memory_space=pltpu.VMEM)] * 7,
+        scratch_shapes=scratch,
+        compiler_params=pltpu.CompilerParams(
+            collective_id=0, has_side_effects=True, vmem_limit_bytes=48 * 1024 * 1024
+        ),
+        name="advection_step",
+    )(*[pltpu.with_memory_space_constraint(arg, pltpu.HBM) for arg in args])
+    results = list(
         pl.pallas_call(
-            functools.partial(kernel, bands, levs, loss_scale),
+            write_out,
             out_shape=out_shape,
-            in_specs=[pl.BlockSpec(memory_space=pltpu.VMEM)] * 11,
-            out_specs=[pl.BlockSpec(memory_space=pltpu.VMEM)] * 7,
-            scratch_shapes=scratch,
-            compiler_params=pltpu.CompilerParams(
-                collective_id=0, has_side_effects=True, vmem_limit_bytes=48 * 1024 * 1024
-            ),
-            name="advection_step",
-        )(*args)
+            in_specs=[pl.BlockSpec(memory_space=pltpu.VMEM)] * 7,
+            out_specs=[pl.BlockSpec(memory_space=pltpu.HBM)] * 7,
+            scratch_shapes=[pltpu.SemaphoreType.DMA((7,))],
+            compiler_params=pltpu.CompilerParams(vmem_limit_bytes=1024 * 1024),
+            name="write_out",
+        )(*results)
     )
+    results[1] = jnp.transpose(results[1], (1, 0, 2))
+    return tuple(results)
+
+
+def write_out(*refs):
+    sem = refs[14]
+    copies = [pltpu.make_async_copy(refs[i], refs[7 + i], sem.at[i]) for i in range(7)]
+    for copy in copies:
+        copy.start()
+    for copy in copies:
+        copy.wait()
 
 
 def solution(mesh):

time: 85.9 us -> 71.6 us (0.83)
  Pallas kernels: 79.1 us -> 70.8 us
  local copies, waits for them, and re-layouts: 5.87 us -> 0 us
    pallas_call x1, Pallas kernels: 79.1 us -> 70.1 us  [on_device(): pl.pallas_call(functools.partial(kernel, bands, levs, loss_scale), out_sh...]
    unnamed x27 -> x0, local copies, waits for them, and re-layouts: 5.25 us -> none
where the time goes in v2:
time: 71.6 us; the launch traced here: 71.5 us
  Pallas kernels  70.8 us (99%)
    pallas_call x1, Pallas kernels, on_device(): pl.pallas_call(functools.partial(kernel, bands, levs, loss_scale), out_sh...  70.1 us

profile of v2, /device:TPU:1, one launch (start us, length us, event | category | flops | bytes accessed | tf_op | source)
XLA Modules:
  0.0 71.5 jit_solution(1753181580364711710)
XLA Ops:
  0.6 70.1 %advection_step.1 = (f32[4,1,2,256]{3,2,1,0:T(2,128)S(1)}, f32[20,2,128]{2,1,0:T(2,128)S(1)}, f32[2,128]{1,0:T(2,128)S(1)}, f32[2,128,128]{2,1,0:T(8,128)S(1)}, ...) custom-call(f32[4,1,2,256]{3,2,1,0:T(2,128)} %conc_hbm.1, f32[4,1,2,256]{3,2,1,0:T(2,128)} %target_hbm.1, ...), custom_call_target="tpu_custom_call" | custom-call | tf_op jit(solution)/shard_map/advection_step/pallas_call | solution.py:841
  70.7 0.7 %write_out.1 = (f32[4,1,2,256]{3,2,1,0:T(2,128)}, f32[20,2,128]{2,1,0:T(2,128)}, f32[2,128]{1,0:T(2,128)}, f32[2,128,128]{2,1,0:T(8,128)}, f32[2,128]{1,0:T(2,12...) custom-call(f32[4,1,2,256]{3,2,1,0:T(2,128)S(1)} %get-tuple-element.21.refs_0_, f32[20,2,128]{2,1,0:T(2,128)S(1)} %get-tuple-element.22.refs_1_, ...), custom_call_target="tpu_custom_call" | custom-call | tf_op jit(solution)/shard_map/write_out/pallas_call | solution.py:853

commit v3 on v2

--- a/solution.py
+++ b/solution.py
@@ -1,3 +1,4 @@
+import contextlib
 import functools
 import math
 
@@ -12,7 +13,7 @@
 WIDTH = 128
 F32 = jnp.float32
 BF16 = jnp.bfloat16
-MESH = pl.DeviceIdType.MESH
+LOGICAL = pl.DeviceIdType.LOGICAL
 BASE = (-1.0 / 12.0, 7.0 / 12.0, 7.0 / 12.0, -1.0 / 12.0)
 
 NY = 256
@@ -22,6 +23,10 @@
 NM = 5 * NY
 NET_ROWS = 160
 GRAD_ROWS = 2 * NET_ROWS
+
+
+def mark(name):
+    return contextlib.nullcontext()
 
 
 def split(x):
@@ -56,6 +61,10 @@
                     live.discard(i)
         tick += 1
     return results
+
+
+def far_first(n):
+    return sorted(range(1, n), key=lambda d: -min(d, n - d))
 
 
 def low_half(shape):
@@ -135,6 +144,12 @@
     halo,
     ghalo,
     winds,
+    block_out,
+    wind_out,
+    pair_out,
+    pair_in,
+    final_out,
+    final_in,
     line,
     gline,
     ax_z,
@@ -155,8 +170,6 @@
     d2_m,
     pb_z,
     pb_m,
-    acc2,
-    acc1,
     acc3,
     accb2,
     accp,
@@ -173,29 +186,40 @@
     ghalo_recv,
     wind_send,
     wind_recv,
+    swap_send,
+    swap_recv,
     red_send,
     red_recv,
-    first_send,
-    first_recv,
 ):
     side_y = math.isqrt(bands)
     side_z = bands // side_y
     band = lax.axis_index("band")
     lev = lax.axis_index("lev")
-    my_y = band // side_z
-    my_z = band % side_z
+    my_y = lax.div(band, side_z)
+    my_z = lax.rem(band, side_z)
+
+    def place(b):
+        y = lax.div(b, side_z)
+        z = b - y * side_z
+        return b + lax.rem(y, 2) * (side_z - 1 - 2 * z)
+
+    mine = place(band)
+    moved = mine != band
+
+    def wrap(at, n):
+        return jnp.where(at >= n, at - n, at)
 
     def y_device(ty):
-        return {"band": ty * side_z + my_z, "lev": lev}
+        return (ty * side_z + my_z) * levs + lev
 
     def z_device(tz):
-        return {"band": my_y * side_z + tz, "lev": lev}
+        return (my_y * side_z + tz) * levs + lev
 
     def lev_device(tl):
-        return {"band": band, "lev": tl}
+        return band * levs + tl
 
     def band_device(tb):
-        return {"band": tb, "lev": lev}
+        return tb * levs + lev
 
     inputs = [
         pltpu.make_async_copy(src, dst, input_sem.at[i])
@@ -223,26 +247,45 @@
     ghalo[...] = jnp.zeros_like(ghalo)
     barrier = pltpu.get_barrier_semaphore()
     greeted = 0
-    for delta in (1, bands - 1, 2, bands - 2):
-        pl.semaphore_signal(
-            barrier, inc=1, device_id=band_device((band + delta) % bands), device_id_type=MESH
-        )
-        greeted += 1
     for d in range(1, levs):
         pl.semaphore_signal(
-            barrier, inc=1, device_id=lev_device((lev + d) % levs), device_id_type=MESH
+            barrier, inc=1, device_id=lev_device(wrap(lev + d, levs)), device_id_type=LOGICAL
         )
         greeted += 1
     for d in range(1, side_y):
         pl.semaphore_signal(
-            barrier, inc=1, device_id=y_device((my_y + d) % side_y), device_id_type=MESH
+            barrier, inc=1, device_id=y_device(wrap(my_y + d, side_y)), device_id_type=LOGICAL
         )
         greeted += 1
     for d in range(1, side_z):
         pl.semaphore_signal(
-            barrier, inc=1, device_id=z_device((my_z + d) % side_z), device_id_type=MESH
+            barrier, inc=1, device_id=z_device(wrap(my_z + d, side_z)), device_id_type=LOGICAL
         )
         greeted += 1
+
+    near_end = (my_z < 2) | (my_z >= side_z - 2)
+
+    def others():
+        for delta in (1, -1, 2, -2):
+            for base, mapped in ((band, True), (mine, False), (mine, True)):
+                at = base + delta
+                known = (at >= 0) & (at < bands)
+                at = jnp.clip(at, 0, bands - 1)
+                device = place(at) if mapped else at
+                yield device, near_end & known & (lax.div(device, side_z) != my_y)
+
+    @pl.when(near_end)
+    def _():
+        for device, other in others():
+
+            @pl.when(other)
+            def _():
+                pl.semaphore_signal(
+                    barrier, inc=1, device_id=band_device(device), device_id_type=LOGICAL
+                )
+
+    for _, other in others():
+        greeted = greeted + other.astype(jnp.int32)
 
     def prepare(net):
         w1 = w1_ref[:, net, :]
@@ -288,7 +331,7 @@
         base = jnp.where((place == 0) | (place == 3), BASE[0], BASE[1])
         b3s[net] = column + base
 
-    def constant_rows(ref, lo_lane, courant, low, high):
+    def constant_rows(ref, lo_lane, courant, low, high, steps):
         n = courant.shape[1]
         place = lax.broadcasted_iota(jnp.int32, (16, n), 0)
         rows = jnp.where(place == 0, courant, 0.0)
@@ -297,7 +340,7 @@
         rows = jnp.where(place == 3, high, rows)
         rows = jnp.where(place == 4, 1.0, rows)
         hi, lo = split(rows)
-        for s in range(STEPS):
+        for s in steps:
             ref[s, 272:288, lo_lane : lo_lane + n] = hi
             ref[s, 304:320, lo_lane : lo_lane + n] = lo
             ref[s, 336:352, lo_lane : lo_lane + n] = hi
@@ -333,7 +376,7 @@
         half = terms[0:8] + terms[8:16]
         return courant * (half + turn(half))
 
-    def backward(net, s, lanes, dflux, courant, d1, d2, pb, s1, s2, st, cf):
+    def backward(net, s, lanes, dflux, courant, d1, d2, pb, s1, s2, st, cf, last=False):
         dq = courant * dflux
         dq = jnp.concatenate([dq, dq], 0)
         weighted = dq * st[s, :, lanes]
@@ -352,6 +395,8 @@
         one = (out[0:128] + out[128:256]) * s1[s, :, lanes]
         pair = stack(one)
         d1[:, lanes] = pair
+        if last:
+            return None, weighted
         yield
         out = dot(w1b[net], pair)
         yield
@@ -362,10 +407,10 @@
 
     def weight_grads(net, s, lanes, ax, h2, d1, d2, pb):
         out = dot_nt(ax[s, 0:288, lanes], d2[:, lanes])
-        acc2[net] += quads(out, 128, 128)
+        grads[net * NET_ROWS : net * NET_ROWS + 128] += quads(out, 128, 128)
         accb2[net] += out[256:288, 0:128] + out[256:288, 128:256]
         out = dot_nt(ax[s, 256:320, lanes], d1[:, lanes])
-        acc1[net] += quads(out, 32, 128)
+        grads[net * NET_ROWS + 128 : (net + 1) * NET_ROWS] += quads(out, 32, 128)
         out = dot_nt(pb[:, lanes], h2[s, :, lanes])
         acc3[net] += quads(out, 16, 128)
 
@@ -395,7 +440,7 @@
         )
         flux = jnp.concatenate(parts, 1)
         new = line[...] - (flux - lane_roll(flux, 1))
-        halo[s, 2] = pick(*from_line(new))
+        return pick(*from_line(new))
 
     def face_stencil(s, face):
         mid = turn(halo[s, 2])
@@ -432,105 +477,218 @@
             )
         return run(fluxes)
 
+    routes = ((1, 1), (-1, 3), (2, 0), (-2, 4))
+
+    def inside(b):
+        return (b >= 0) & (b < bands)
+
     def halo_copy(buf, s, which, send, recv):
-        delta, slot = ((1, 1), (-1, 3), (2, 0), (-2, 4))[which]
+        delta, slot = routes[which]
         return pltpu.make_async_remote_copy(
             src_ref=buf.at[s, 2],
             dst_ref=buf.at[s, slot],
-            send_sem=send.at[s, which],
+            send_sem=send.at[which],
             recv_sem=recv.at[s, which],
-            device_id=band_device(band + delta),
-            device_id_type=MESH,
-        )
-
-    has_target = (band < bands - 1, band >= 1, band < bands - 2, band >= 2)
-    has_source = (band >= 1, band < bands - 1, band >= 2, band < bands - 2)
+            device_id=band_device(place(jnp.clip(mine + delta, 0, bands - 1))),
+            device_id_type=LOGICAL,
+        )
 
     def halo_start(buf, s, send, recv, which_all):
         for which in which_all:
 
-            @pl.when(has_target[which])
+            @pl.when(inside(mine + routes[which][0]))
             def _():
                 halo_copy(buf, s, which, send, recv).start()
 
     def halo_wait(buf, s, send, recv, which_all):
         for which in which_all:
 
-            @pl.when(has_source[which])
+            @pl.when(inside(mine - routes[which][0]))
             def _():
                 halo_copy(buf, s, which, send, recv).wait_recv()
 
     def halo_drain(buf, s, send, recv, which_all):
         for which in which_all:
 
-            @pl.when(has_target[which])
+            @pl.when(inside(mine + routes[which][0]))
             def _():
                 halo_copy(buf, s, which, send, recv).wait_send()
+
+    def move_copy(src, buf, which, send, recv):
+        delta, slot = routes[which] if which < 4 else (0, 2)
+        return pltpu.make_async_remote_copy(
+            src_ref=src,
+            dst_ref=buf.at[0, slot],
+            send_sem=send.at[which],
+            recv_sem=recv.at[0, which],
+            device_id=band_device(place(jnp.clip(band + delta, 0, bands - 1))),
+            device_id_type=LOGICAL,
+        )
+
+    def move_delta(which):
+        return routes[which][0] if which < 4 else 0
+
+    def move_start(src, buf, send, recv, which_all):
+        for which in which_all:
+            delta = move_delta(which)
+            here = band + delta == mine
+
+            @pl.when(inside(band + delta) & jnp.logical_not(here))
+            def _():
+                move_copy(src, buf, which, send, recv).start()
+
+            @pl.when(here)
+            def _():
+                buf[0, routes[which][1] if which < 4 else 2] = src[...]
+
+    def move_wait(src, buf, send, recv, which_all):
+        for which in which_all:
+            delta = move_delta(which)
+
+            @pl.when(inside(mine - delta) & (mine - delta != band))
+            def _():
+                move_copy(src, buf, which, send, recv).wait_recv()
+
+    def move_drain(src, buf, send, recv, which_all):
+        for which in which_all:
+            delta = move_delta(which)
+
+            @pl.when(inside(band + delta) & (band + delta != mine))
+            def _():
+                move_copy(src, buf, which, send, recv).wait_send()
+
+    def swap_copy(src, dst, index):
+        return pltpu.make_async_remote_copy(
+            src_ref=src,
+            dst_ref=dst,
+            send_sem=swap_send.at[index],
+            recv_sem=swap_recv.at[index],
+            device_id=band_device(mine),
+            device_id_type=LOGICAL,
+        )
 
     for copy in inputs:
         copy.wait()
-    prepare(0)
-    rows = [conc_ref[b, 0, r : r + 1, :] for r in range(2) for b in range(4)]
-    line[...] = to_line(*both_rows(jnp.concatenate(rows, 0)))
-    sea = sea_ref[...].astype(F32)
-    zw = to_line(zwind_ref[0, 0:1, :], zwind_ref[0, 1:2, :])
-    zs = to_line(sea[0:1, :], sea[1:2, :])
-    courant = 0.5 * (zw + lane_roll(zw, -1))
-    zcour[...] = jnp.broadcast_to(courant, (8, NZ))
-    constant_rows(ax_z, 0, courant, zs, lane_roll(zs, -1))
-    winds[0, 2, 0:2, :] = mwind_ref[0]
-    winds[0, 2, 2:4, :] = sea
-    for acc in (acc2, acc1, acc3, accb2, accp):
-        acc[...] = jnp.zeros_like(acc)
+    def block_of(ref):
+        rows = [ref[b, 0, r : r + 1, :] for r in range(2) for b in range(4)]
+        return jnp.concatenate(rows, 0)
+
+    def zonal_constants(slab, steps):
+        zw = to_line(slab[4:5, :], slab[5:6, :])
+        zs = to_line(slab[2:3, :], slab[3:4, :])
+        courant = 0.5 * (zw + lane_roll(zw, -1))
+        zcour[...] = jnp.broadcast_to(courant, (8, NZ))
+        constant_rows(ax_z, 0, courant, zs, lane_roll(zs, -1), steps)
+
+    with mark("prepare"):
+        prepare(0)
+        pair_out[0] = block_of(conc_ref)
+        pair_out[1] = block_of(target_ref)
+        slab = jnp.concatenate(
+            [mwind_ref[0], sea_ref[...].astype(F32), zwind_ref[0], zwind_ref[0]], 0
+        )
+        wind_out[...] = slab
+        line[...] = to_line(*both_rows(pair_out[0]))
+        zonal_constants(slab, range(STEPS))
+        for acc in (grads, acc3, accb2, accp):
+            acc[...] = jnp.zeros_like(acc)
+    with mark("zonal"):
+        block_out[...] = zonal(0)
+    with mark("barrier"):
+        pl.semaphore_wait(barrier, greeted)
+    move_start(block_out, halo, halo_send, halo_recv, (0, 1, 4))
+    move_start(wind_out, winds, wind_send, wind_recv, (0, 1, 4))
+    move_start(block_out, halo, halo_send, halo_recv, (2, 3))
+
+    @pl.when(moved)
+    def _():
+        swap_copy(pair_out, pair_in, 0).start()
+
+    @pl.when(jnp.logical_not(moved))
+    def _():
+        pair_in[...] = pair_out[...]
+
+    with mark("prepare1"):
+        prepare(1)
+    with mark("waitwind"):
+        move_wait(wind_out, winds, wind_send, wind_recv, (0, 1, 4))
+    with mark("constants"):
+        w = [winds[0, 1 + i // 2, i % 2 : i % 2 + 1, :] for i in range(6)]
+        m = [winds[0, 1 + i // 2, 2 + i % 2 : 3 + i % 2, :] for i in range(6)]
+        for slot, face in enumerate(SLOT_FACE):
+            courant = 0.5 * (w[face] + w[face + 1])
+            mcour[:, slot * NY : (slot + 1) * NY] = jnp.broadcast_to(courant, (8, NY))
+            constant_rows(ax_m, slot * NY, courant, m[face], m[face + 1], range(STEPS))
+
+        @pl.when(moved)
+        def _():
+            zonal_constants(winds[0, 2], range(STEPS))
+
+    with mark("waitmove"):
+        move_wait(block_out, halo, halo_send, halo_recv, (0, 1, 4))
+
+    def merid(s):
+        with mark("merid"):
+            f1, f2, f3 = merid_faces(s, (0, 1, 2))
+            new = halo[s, 2] - pick(f2 - f1, f3 - f2)
+            line[...] = to_line(*both_rows(new))
+        return new
+
+    move_drain(block_out, halo, halo_send, halo_recv, (0, 1, 2, 3, 4))
+    merid(0)
 
     def forward_step(s, carry):
-        zonal(s)
-
-        @pl.when(s == 0)
-        def _():
-            pl.semaphore_wait(barrier, greeted)
-            halo_start(winds, 0, wind_send, wind_recv, (0, 1))
-
+        with mark("zonal"):
+            halo[s, 2] = zonal(s)
         halo_start(halo, s, halo_send, halo_recv, (0, 1, 2, 3))
 
-        @pl.when(s == 0)
-        def _():
-            prepare(1)
-            halo_wait(winds, 0, wind_send, wind_recv, (0, 1))
-            w = [winds[0, 1 + i // 2, i % 2 : i % 2 + 1, :] for i in range(6)]
-            m = [winds[0, 1 + i // 2, 2 + i % 2 : 3 + i % 2, :] for i in range(6)]
-            for slot, face in enumerate(SLOT_FACE):
-                courant = 0.5 * (w[face] + w[face + 1])
-                mcour[:, slot * NY : (slot + 1) * NY] = jnp.broadcast_to(courant, (8, NY))
-                constant_rows(ax_m, slot * NY, courant, m[face], m[face + 1])
-
-        @pl.when(s > 0)
-        def _():
-            halo_wait(halo, s - 1, halo_send, halo_recv, (2, 3))
+        with mark("redundant"):
+
+            @pl.when(s == 1)
+            def _():
+                move_wait(block_out, halo, halo_send, halo_recv, (2, 3))
+
+            @pl.when(s > 1)
+            def _():
+                halo_wait(halo, s - 1, halo_send, halo_recv, (2, 3))
+
             merid_faces(s - 1, (3, 4))
-
-        halo_wait(halo, s, halo_send, halo_recv, (0, 1))
-        f1, f2, f3 = merid_faces(s, (0, 1, 2))
-        new = halo[s, 2] - pick(f2 - f1, f3 - f2)
-        line[...] = to_line(*both_rows(new))
+        with mark("waithalo"):
+            halo_wait(halo, s, halo_send, halo_recv, (0, 1))
+        halo_drain(halo, s, halo_send, halo_recv, (0, 1, 2, 3))
+        new = merid(s)
 
         @pl.when(s == STEPS - 1)
         def _():
-            rows = [target_ref[b, 0, r : r + 1, :] for r in range(2) for b in range(4)]
-            ghalo[STEPS - 1, 2] = (new - jnp.concatenate(rows, 0)) * loss_scale
+            @pl.when(moved)
+            def _():
+                swap_copy(pair_out, pair_in, 0).wait_recv()
+
+            ghalo[STEPS - 1, 2] = (new - pair_in[1]) * loss_scale
             halo_start(ghalo, STEPS - 1, ghalo_send, ghalo_recv, (0, 1))
-            for r in range(2):
-                for b in range(4):
-                    field_ref[b, 0, r : r + 1, :] = new[4 * r + b : 4 * r + b + 1, :]
+            final_out[...] = new
+
+            @pl.when(moved)
+            def _():
+                swap_copy(final_out, final_in, 1).start()
 
         return carry
 
-    lax.fori_loop(0, STEPS, forward_step, 0)
-    halo_wait(halo, STEPS - 1, halo_send, halo_recv, (2, 3))
-    merid_faces(STEPS - 1, (3, 4))
+    lax.fori_loop(1, STEPS, forward_step, 0)
+    with mark("redundant"):
+        halo_wait(halo, STEPS - 1, halo_send, halo_recv, (2, 3))
+        merid_faces(STEPS - 1, (3, 4))
+
+    @pl.when(moved)
+    def _():
+        with mark("zonal_again"):
+            line[...] = to_line(*both_rows(pair_in[0]))
+            zonal(0)
 
     def merid_back(s):
-        halo_wait(ghalo, s, ghalo_send, ghalo_recv, (0, 1))
+        with mark("waitg"):
+            halo_wait(ghalo, s, ghalo_send, ghalo_recv, (0, 1))
+        halo_drain(ghalo, s, ghalo_send, ghalo_recv, (0, 1))
         g = []
         for block in (1, 2, 3):
             g.extend(both_rows(ghalo[s, block]))
@@ -568,13 +726,13 @@
         new = new + turn(pick(highs[2] + lows[4], highs[0] + lows[2]))
         accp[1] += inner
 
-        @pl.when(band == 0)
+        @pl.when(mine == 0)
         def _():
             accp[1] += first
 
         gline[...] = to_line(*both_rows(new))
 
-    def zonal_back(s):
+    def zonal_back(s, last=False):
         gz = gline[...]
         dflux = lane_roll(gz, -1) - gz
         outs = run(
@@ -592,22 +750,25 @@
                     s2_z,
                     st_z,
                     cf_z,
+                    last,
                 )
                 for lanes in zchunks
             ]
         )
+        accp[0] += sum(lane_fold(o[1]) for o in outs)
+        if last:
+            return None
         out = jnp.concatenate([o[0] for o in outs], 1)
         low, high = out[0:8], out[8:16]
         t = pick(lane_roll(low, -1), low) + pick(lane_roll(high, 1), lane_roll(high, 2))
         new = gz + t + turn(t)
 
-        accp[0] += sum(lane_fold(o[1]) for o in outs)
         return pick(*from_line(new))
 
     def merid_weights(s):
         weight_grads(1, s, slice(NY, 3 * NY), ax_m, h2_m, d1_m, d2_m, pb_m)
 
-        @pl.when(band == 0)
+        @pl.when(mine == 0)
         def _():
             weight_grads(1, s, slice(0, NY), ax_m, h2_m, d1_m, d2_m, pb_m)
 
@@ -619,8 +780,9 @@
         merid_back(s)
         ghalo[s - 1, 2] = zonal_back(s)
         halo_start(ghalo, s - 1, ghalo_send, ghalo_recv, (0, 1))
-        merid_weights(s)
-        zonal_weights(s)
+        with mark("weights"):
+            merid_weights(s)
+            zonal_weights(s)
         return carry
 
     lax.fori_loop(0, STEPS - 1, backward_step, 0)
@@ -635,8 +797,6 @@
 
     def gather_net(net):
         top = net * NET_ROWS
-        grads[top : top + 128] = acc2[net]
-        grads[top + 128 : top + 160] = acc1[net]
         grads[top + 149 : top + 150] = accb2[net, 20:21, :]
         grads[top + 152 : top + 156] = dot(centre, stack(acc3[net]))[0:4]
         sums = jnp.sum(accp[net], 1, keepdims=True)
@@ -651,110 +811,106 @@
     part = piece // side_y
     started = []
 
-    def send(src, dst, index, device):
-        copy = pltpu.make_async_remote_copy(
+    def send(src, dst, phase, device):
+        pltpu.make_async_remote_copy(
             src_ref=src,
             dst_ref=dst,
-            send_sem=red_send.at[index],
-            recv_sem=red_recv.at[index],
+            send_sem=red_send.at[phase],
+            recv_sem=red_recv.at[phase],
             device_id=device,
-            device_id_type=MESH,
-        )
-        copy.start()
-        started.append(copy)
-        return copy
-
-    def wait(copies):
-        for copy in copies:
-            copy.wait_recv()
+            device_id_type=LOGICAL,
+        ).start()
+
+    def wait(buf, count, phase):
+        with mark("wait_ar"):
+            some = buf.at[0:count]
+            pltpu.make_async_copy(some, some, red_recv.at[phase]).wait()
+        started.append((some, phase))
 
     wide = levs // 2
-    core = lev % 2
-    my_x = lev // 2
+    my_x = lax.div(lev, 2)
+    core = lev - 2 * my_x
 
     def first_copy(net, k):
-        tx = (my_x + k) % wide
+        tx = wrap(my_x + k, wide)
         slot = 2 * k + core
         row = pl.multiple_of(net * NET_ROWS + tx * piece, 8)
         return pltpu.make_async_remote_copy(
             src_ref=grads.at[pl.ds(row, piece)],
             dst_ref=r1.at[slot],
-            send_sem=first_send.at[net, k],
-            recv_sem=first_recv.at[slot],
+            send_sem=red_send.at[0],
+            recv_sem=red_recv.at[0],
             device_id=lev_device(2 * tx + net),
-            device_id_type=MESH,
+            device_id_type=LOGICAL,
         )
 
     def send_net(net):
-        for k in range(wide - 1, 0, -1):
+        for k in far_first(wide):
             first_copy(net, k).start()
 
         @pl.when(core != net)
         def _():
             first_copy(net, 0).start()
 
-    def drain_net(net):
+    merid_back(0)
+    with mark("wg1"):
+        merid_weights(0)
+    with mark("gather1"):
+        gather_net(1)
+        send_net(1)
+    with mark("zback0"):
+        zonal_back(0, True)
+    with mark("wg0"):
+        zonal_weights(0)
+    with mark("gather0"):
+        gather_net(0)
+        send_net(0)
+    @pl.when(moved)
+    def _():
+        swap_copy(final_out, final_in, 1).wait()
+        swap_copy(pair_out, pair_in, 0).wait_send()
+
+    final = jnp.where(moved, final_in[...], final_out[...])
+    for r in range(2):
+        for b in range(4):
+            field_ref[b, 0, r : r + 1, :] = final[4 * r + b : 4 * r + b + 1, :]
+    move_drain(wind_out, winds, wind_send, wind_recv, (0, 1, 4))
+
+    row = pl.multiple_of(core * NET_ROWS + my_x * piece, 8)
+    with mark("wait_ar"):
+        wait(r1, levs - 1, 0)
+        total = grads[pl.ds(row, piece)] + r1[1 - core]
         for k in range(1, wide):
-            first_copy(net, k).wait_send()
-
-        @pl.when(core != net)
-        def _():
-            first_copy(net, 0).wait_send()
-
-    def arrived(slot):
-        pltpu.make_async_copy(r1.at[slot], r1.at[slot], first_recv.at[slot]).wait()
-        return r1[slot]
-
-    merid_back(0)
-    merid_weights(0)
-    gather_net(1)
-    send_net(1)
-    zonal_back(0)
-    zonal_weights(0)
-    gather_net(0)
-    send_net(0)
-    row = pl.multiple_of(core * NET_ROWS + my_x * piece, 8)
-    total = grads[pl.ds(row, piece)] + arrived(1 - core)
-    for k in range(1, wide):
-        for c in range(2):
-            total = total + arrived(2 * k + c)
-    at = 0
+            for c in range(2):
+                total = total + r1[2 * k + c]
     for i in range(side_y):
         s1buf[i] = total[i * part : (i + 1) * part]
-    copies = []
-    for d in range(1, side_y):
-        ty = (my_y + d) % side_y
-        copies.append(send(s1buf.at[ty], r2.at[d - 1], at, y_device(ty)))
-        at += 1
+    for d in far_first(side_y):
+        ty = wrap(my_y + d, side_y)
+        send(s1buf.at[ty], r2.at[d - 1], 1, y_device(ty))
     total = s1buf[my_y]
-    wait(copies)
+    wait(r2, side_y - 1, 1)
     for d in range(1, side_y):
         total = total + r2[d - 1]
     r3[my_z] = total
-    copies = []
-    for d in range(1, side_z):
-        tz = (my_z + d) % side_z
-        copies.append(send(r3.at[my_z], r3.at[my_z], at, z_device(tz)))
-        at += 1
-    wait(copies)
+    for d in far_first(side_z):
+        tz = wrap(my_z + d, side_z)
+        send(r3.at[my_z], r3.at[my_z], 2, z_device(tz))
+    wait(r3, side_z - 1, 2)
     total = r3[0]
     for i in range(1, side_z):
         total = total + r3[i]
     a4[my_y] = total
-    copies = []
-    for d in range(1, side_y):
-        ty = (my_y + d) % side_y
-        copies.append(send(a4.at[my_y], a4.at[my_y], at, y_device(ty)))
-        at += 1
-    wait(copies)
+    for d in far_first(side_y):
+        ty = wrap(my_y + d, side_y)
+        send(a4.at[my_y], a4.at[my_y], 3, y_device(ty))
+    wait(a4, side_y - 1, 3)
     for i in range(side_y):
         full[lev, i * part : (i + 1) * part] = a4[i]
-    copies = []
-    for d in range(1, levs):
-        tl = (lev + d) % levs
-        copies.append(send(full.at[lev], full.at[lev], at, lev_device(tl)))
-        at += 1
-    wait(copies)
+    for d in sorted(range(1, levs), key=lambda d: -min(d // 2, wide - d // 2)):
+        tl = wrap(lev + d, levs)
+        send(full.at[lev], full.at[lev], 4, lev_device(tl))
+    wait(full, levs - 1, 4)
     for net in range(2):
         everything = jnp.concatenate([full[2 * x + net] for x in range(wide)], 0)
         top = 0
@@ -765,14 +921,8 @@
         gw3_ref[net] = everything[top + 152 : top + 156]
         gb3_ref[net : net + 1] = everything[top + 156 : top + 157, 0:4]
 
-    for copy in started:
-        copy.wait_send()
-    drain_net(0)
-    drain_net(1)
-    halo_drain(winds, 0, wind_send, wind_recv, (0, 1))
-    for s in range(STEPS):
-        halo_drain(halo, s, halo_send, halo_recv, (0, 1, 2, 3))
-        halo_drain(ghalo, s, ghalo_send, ghalo_recv, (0, 1))
+    for some, phase in started:
+        pltpu.make_async_copy(some, some, red_send.at[phase]).wait()
 
 
 def on_device(bands, levs, loss_scale, *args):
@@ -780,7 +930,6 @@
     side_y = math.isqrt(bands)
     side_z = bands // side_y
     part = piece // side_y
-    reductions = (levs - 1) + 2 * (side_y - 1) + (side_z - 1)
     vmem = pltpu.VMEM
     sweeps = [NZ, NM]
     args = list(args)
@@ -801,6 +950,12 @@
         vmem((STEPS, 5, 8, NY), F32),
         vmem((STEPS, 5, 8, NY), F32),
         vmem((1, 5, 8, NY), F32),
+        vmem((8, NY), F32),
+        vmem((8, NY), F32),
+        vmem((2, 8, NY), F32),
+        vmem((2, 8, NY), F32),
+        vmem((8, NY), F32),
+        vmem((8, NY), F32),
         vmem((8, NZ), F32),
         vmem((8, NZ), F32),
         *[vmem((STEPS, 352, n), BF16) for n in sweeps],
@@ -812,8 +967,6 @@
         *[vmem((256, n), BF16) for n in sweeps],
         *[vmem((256, n), BF16) for n in sweeps],
         *[vmem((32, n), BF16) for n in sweeps],
-        vmem((2, 128, 128), F32),
-        vmem((2, 32, 128), F32),
         vmem((2, 16, 128), F32),
         vmem((2, 32, 128), F32),
         vmem((2, 16, 128), F32),
@@ -824,16 +977,16 @@
         vmem((side_z, part, 128), F32),
         vmem((side_y, part, 128), F32),
         vmem((levs, piece, 128), F32),
-        pltpu.SemaphoreType.DMA((STEPS, 4)),
-        pltpu.SemaphoreType.DMA((STEPS, 4)),
-        pltpu.SemaphoreType.DMA((STEPS, 4)),
-        pltpu.SemaphoreType.DMA((STEPS, 4)),
-        pltpu.SemaphoreType.DMA((1, 4)),
-        pltpu.SemaphoreType.DMA((1, 4)),
-        pltpu.SemaphoreType.DMA((reductions,)),
-        pltpu.SemaphoreType.DMA((reductions,)),
-        pltpu.SemaphoreType.DMA((2, levs // 2)),
-        pltpu.SemaphoreType.DMA((levs,)),
+        pltpu.SemaphoreType.DMA((5,)),
+        pltpu.SemaphoreType.DMA((STEPS, 5)),
+        pltpu.SemaphoreType.DMA((2,)),
+        pltpu.SemaphoreType.DMA((STEPS, 2)),
+        pltpu.SemaphoreType.DMA((5,)),
+        pltpu.SemaphoreType.DMA((1, 5)),
+        pltpu.SemaphoreType.DMA((2,)),
+        pltpu.SemaphoreType.DMA((2,)),
+        pltpu.SemaphoreType.DMA((5,)),
+        pltpu.SemaphoreType.DMA((5,)),
     ]
     out_shape = [jax.ShapeDtypeStruct(args[0].shape, F32)] + [
         jax.ShapeDtypeStruct(args[i].shape, F32) for i in range(5, 11)

time: 71.6 us -> 67.4 us (0.941)
  Pallas kernels: 70.8 us -> 66.6 us
    pallas_call x1, Pallas kernels: 70.1 us -> 65.8 us  [on_device(): pl.pallas_call(functools.partial(kernel, bands, levs, loss_scale), out_sh...]
where the time goes in v3:
time: 67.4 us; the launch traced here: 67.2 us
  Pallas kernels  66.6 us (99%)
    pallas_call x1, Pallas kernels, on_device(): pl.pallas_call(functools.partial(kernel, bands, levs, loss_scale), out_sh...  65.8 us

profile of v3, /device:TPU:1, one launch (start us, length us, event | category | flops | bytes accessed | tf_op | source)
XLA Modules:
  0.0 67.2 jit_solution(7646568309719752130)
XLA Ops:
  0.6 65.8 %advection_step.1 = (f32[4,1,2,256]{3,2,1,0:T(2,128)S(1)}, f32[20,2,128]{2,1,0:T(2,128)S(1)}, f32[2,128]{1,0:T(2,128)S(1)}, f32[2,128,128]{2,1,0:T(8,128)S(1)}, ...) custom-call(f32[4,1,2,256]{3,2,1,0:T(2,128)} %conc_hbm.1, f32[4,1,2,256]{3,2,1,0:T(2,128)} %target_hbm.1, ...), custom_call_target="tpu_custom_call" | custom-call | tf_op jit(solution)/shard_map/advection_step/pallas_call | solution.py:994
  66.5 0.7 %write_out.1 = (f32[4,1,2,256]{3,2,1,0:T(2,128)}, f32[20,2,128]{2,1,0:T(2,128)}, f32[2,128]{1,0:T(2,128)}, f32[2,128,128]{2,1,0:T(8,128)}, f32[2,128]{1,0:T(2,12...) custom-call(f32[4,1,2,256]{3,2,1,0:T(2,128)S(1)} %get-tuple-element.21.refs_0_, f32[20,2,128]{2,1,0:T(2,128)S(1)} %get-tuple-element.22.refs_1_, ...), custom_call_target="tpu_custom_call" | custom-call | tf_op jit(solution)/shard_map/write_out/pallas_call | solution.py:1006

commit v4 on v3

--- a/solution.py
+++ b/solution.py
@@ -19,8 +19,9 @@
 NY = 256
 GAP = 64
 NZ = 640
-SLOT_FACE = (1, 2, 3, 0, 4)
-NM = 5 * NY
+SLOT_FACE = (1, 2, 3, 0, 4, -1, 5)
+NM = 7 * NY
+NB = 5 * NY
 NET_ROWS = 160
 GRAD_ROWS = 2 * NET_ROWS
 
@@ -146,8 +147,10 @@
     winds,
     block_out,
     wind_out,
-    pair_out,
-    pair_in,
+    conc_out,
+    conc_in,
+    target_out,
+    targets,
     final_out,
     final_in,
     line,
@@ -186,6 +189,8 @@
     ghalo_recv,
     wind_send,
     wind_recv,
+    target_send,
+    target_recv,
     swap_send,
     swap_recv,
     red_send,
@@ -245,6 +250,7 @@
     winds[...] = jnp.zeros_like(winds)
     halo[...] = jnp.zeros_like(halo)
     ghalo[...] = jnp.zeros_like(ghalo)
+    targets[...] = jnp.zeros_like(targets)
     barrier = pltpu.get_barrier_semaphore()
     greeted = 0
     for d in range(1, levs):
@@ -446,6 +452,10 @@
         mid = turn(halo[s, 2])
         if face == 1:
             return jnp.concatenate([halo[s, 1], halo[s, 2]], 0)
+        if face == -1:
+            return jnp.concatenate([halo[s, 0], halo[s, 1]], 0)
+        if face == 5:
+            return jnp.concatenate([halo[s, 3], halo[s, 4]], 0)
         if face == 3:
             return jnp.concatenate([halo[s, 2], halo[s, 3]], 0)
         if face == 2:
@@ -580,15 +590,26 @@
         zcour[...] = jnp.broadcast_to(courant, (8, NZ))
         constant_rows(ax_z, 0, courant, zs, lane_roll(zs, -1), steps)
 
+    def merid_constants(slots, steps):
+        def row(i, at):
+            block, which = (i + 1) // 2, at + (i + 1) % 2
+            return winds[0, block, which : which + 1, :]
+
+        for slot in slots:
+            face = SLOT_FACE[slot]
+            courant = 0.5 * (row(face + 1, 0) + row(face + 2, 0))
+            mcour[:, slot * NY : (slot + 1) * NY] = jnp.broadcast_to(courant, (8, NY))
+            constant_rows(ax_m, slot * NY, courant, row(face + 1, 2), row(face + 2, 2), steps)
+
     with mark("prepare"):
         prepare(0)
-        pair_out[0] = block_of(conc_ref)
-        pair_out[1] = block_of(target_ref)
+        conc_out[...] = block_of(conc_ref)
+        target_out[...] = block_of(target_ref)
         slab = jnp.concatenate(
             [mwind_ref[0], sea_ref[...].astype(F32), zwind_ref[0], zwind_ref[0]], 0
         )
         wind_out[...] = slab
-        line[...] = to_line(*both_rows(pair_out[0]))
+        line[...] = to_line(*both_rows(conc_out[...]))
         zonal_constants(slab, range(STEPS))
         for acc in (grads, acc3, accb2, accp):
             acc[...] = jnp.zeros_like(acc)
@@ -599,26 +620,23 @@
     move_start(block_out, halo, halo_send, halo_recv, (0, 1, 4))
     move_start(wind_out, winds, wind_send, wind_recv, (0, 1, 4))
     move_start(block_out, halo, halo_send, halo_recv, (2, 3))
+    move_start(wind_out, winds, wind_send, wind_recv, (2, 3))
+    move_start(target_out, targets, target_send, target_recv, (0, 1, 4))
 
     @pl.when(moved)
     def _():
-        swap_copy(pair_out, pair_in, 0).start()
+        swap_copy(conc_out, conc_in, 0).start()
 
     @pl.when(jnp.logical_not(moved))
     def _():
-        pair_in[...] = pair_out[...]
+        conc_in[...] = conc_out[...]
 
     with mark("prepare1"):
         prepare(1)
     with mark("waitwind"):
         move_wait(wind_out, winds, wind_send, wind_recv, (0, 1, 4))
     with mark("constants"):
-        w = [winds[0, 1 + i // 2, i % 2 : i % 2 + 1, :] for i in range(6)]
-        m = [winds[0, 1 + i // 2, 2 + i % 2 : 3 + i % 2, :] for i in range(6)]
-        for slot, face in enumerate(SLOT_FACE):
-            courant = 0.5 * (w[face] + w[face + 1])
-            mcour[:, slot * NY : (slot + 1) * NY] = jnp.broadcast_to(courant, (8, NY))
-            constant_rows(ax_m, slot * NY, courant, m[face], m[face + 1], range(STEPS))
+        merid_constants((0, 1, 2, 3, 4), range(STEPS))
 
         @pl.when(moved)
         def _():
@@ -637,58 +655,63 @@
     move_drain(block_out, halo, halo_send, halo_recv, (0, 1, 2, 3, 4))
     merid(0)
 
-    def forward_step(s, carry):
+    def halo_step(s):
         with mark("zonal"):
             halo[s, 2] = zonal(s)
         halo_start(halo, s, halo_send, halo_recv, (0, 1, 2, 3))
 
-        with mark("redundant"):
-
-            @pl.when(s == 1)
-            def _():
-                move_wait(block_out, halo, halo_send, halo_recv, (2, 3))
-
-            @pl.when(s > 1)
-            def _():
-                halo_wait(halo, s - 1, halo_send, halo_recv, (2, 3))
-
-            merid_faces(s - 1, (3, 4))
-        with mark("waithalo"):
-            halo_wait(halo, s, halo_send, halo_recv, (0, 1))
-        halo_drain(halo, s, halo_send, halo_recv, (0, 1, 2, 3))
-        new = merid(s)
-
-        @pl.when(s == STEPS - 1)
-        def _():
-            @pl.when(moved)
-            def _():
-                swap_copy(pair_out, pair_in, 0).wait_recv()
-
-            ghalo[STEPS - 1, 2] = (new - pair_in[1]) * loss_scale
-            halo_start(ghalo, STEPS - 1, ghalo_send, ghalo_recv, (0, 1))
-            final_out[...] = new
-
-            @pl.when(moved)
-            def _():
-                swap_copy(final_out, final_in, 1).start()
-
-        return carry
-
-    lax.fori_loop(1, STEPS, forward_step, 0)
+    halo_step(1)
     with mark("redundant"):
-        halo_wait(halo, STEPS - 1, halo_send, halo_recv, (2, 3))
-        merid_faces(STEPS - 1, (3, 4))
+        move_wait(block_out, halo, halo_send, halo_recv, (2, 3))
+        merid_faces(0, (3, 4))
+        move_wait(wind_out, winds, wind_send, wind_recv, (2, 3))
+        merid_constants((5, 6), (STEPS - 1,))
+
+    with mark("waithalo"):
+        halo_wait(halo, 1, halo_send, halo_recv, (0, 1))
+    halo_drain(halo, 1, halo_send, halo_recv, (0, 1, 2, 3))
+    merid(1)
+    halo_step(2)
+    with mark("redundant"):
+        halo_wait(halo, 1, halo_send, halo_recv, (2, 3))
+        merid_faces(1, (3, 4))
 
     @pl.when(moved)
     def _():
         with mark("zonal_again"):
-            line[...] = to_line(*both_rows(pair_in[0]))
+            swap_copy(conc_out, conc_in, 0).wait_recv()
+            line[...] = to_line(*both_rows(conc_in[...]))
             zonal(0)
 
+    move_wait(target_out, targets, target_send, target_recv, (0, 1, 4))
+    with mark("waithalo"):
+        halo_wait(halo, 2, halo_send, halo_recv, (0, 1))
+    halo_drain(halo, 2, halo_send, halo_recv, (0, 1, 2, 3))
+    with mark("merid"):
+        f1, f2, f3 = merid_faces(2, (0, 1, 2))
+    with mark("waittwo"):
+        halo_wait(halo, 2, halo_send, halo_recv, (2, 3))
+    with mark("merid4"):
+        f0, f4, f9, f5 = merid_faces(2, (3, 4, 5, 6))
+    new = halo[2, 2] - pick(f2 - f1, f3 - f2)
+    before = halo[2, 1] - pick(f0 - f9, f1 - f0)
+    after = halo[2, 3] - pick(f4 - f3, f5 - f4)
+    ghalo[2, 2] = (new - targets[0, 2]) * loss_scale
+    ghalo[2, 1] = jnp.where(mine > 0, (before - targets[0, 1]) * loss_scale, 0.0)
+    ghalo[2, 3] = jnp.where(mine < bands - 1, (after - targets[0, 3]) * loss_scale, 0.0)
+    final_out[...] = new
+
+    @pl.when(moved)
+    def _():
+        swap_copy(final_out, final_in, 1).start()
+
     def merid_back(s):
-        with mark("waitg"):
-            halo_wait(ghalo, s, ghalo_send, ghalo_recv, (0, 1))
-        halo_drain(ghalo, s, ghalo_send, ghalo_recv, (0, 1))
+        @pl.when(s < STEPS - 1)
+        def _():
+            with mark("waitg"):
+                halo_wait(ghalo, s, ghalo_send, ghalo_recv, (0, 1))
+            halo_drain(ghalo, s, ghalo_send, ghalo_recv, (0, 1))
+
         g = []
         for block in (1, 2, 3):
             g.extend(both_rows(ghalo[s, block]))
@@ -696,7 +719,7 @@
         first = None
         inner = None
         parts = []
-        for slot, face in enumerate(SLOT_FACE):
+        for slot, face in enumerate(SLOT_FACE[:5]):
             lanes = slice(slot * NY, (slot + 1) * NY)
             part = backward(
                 1,
@@ -868,13 +891,14 @@
     @pl.when(moved)
     def _():
         swap_copy(final_out, final_in, 1).wait()
-        swap_copy(pair_out, pair_in, 0).wait_send()
+        swap_copy(conc_out, conc_in, 0).wait_send()
 
     final = jnp.where(moved, final_in[...], final_out[...])
     for r in range(2):
         for b in range(4):
             field_ref[b, 0, r : r + 1, :] = final[4 * r + b : 4 * r + b + 1, :]
-    move_drain(wind_out, winds, wind_send, wind_recv, (0, 1, 4))
+    move_drain(wind_out, winds, wind_send, wind_recv, (0, 1, 2, 3, 4))
+    move_drain(target_out, targets, target_send, target_recv, (0, 1, 4))
 
     row = pl.multiple_of(core * NET_ROWS + my_x * piece, 8)
     with mark("wait_ar"):
@@ -932,6 +956,7 @@
     part = piece // side_y
     vmem = pltpu.VMEM
     sweeps = [NZ, NM]
+    back = [NZ, NB]
     args = list(args)
     args[5] = jnp.transpose(args[5], (1, 0, 2))
     scratch = [
@@ -952,8 +977,10 @@
         vmem((1, 5, 8, NY), F32),
         vmem((8, NY), F32),
         vmem((8, NY), F32),
-        vmem((2, 8, NY), F32),
-        vmem((2, 8, NY), F32),
+        vmem((8, NY), F32),
+        vmem((8, NY), F32),
+        vmem((8, NY), F32),
+        vmem((1, 5, 8, NY), F32),
         vmem((8, NY), F32),
         vmem((8, NY), F32),
         vmem((8, NZ), F32),
@@ -964,9 +991,9 @@
         *[vmem((STEPS, 128, n), F32) for n in sweeps],
         *[vmem((STEPS, 16, n), F32) for n in sweeps],
         *[vmem((STEPS, 16, n), F32) for n in sweeps],
-        *[vmem((256, n), BF16) for n in sweeps],
-        *[vmem((256, n), BF16) for n in sweeps],
-        *[vmem((32, n), BF16) for n in sweeps],
+        *[vmem((256, n), BF16) for n in back],
+        *[vmem((256, n), BF16) for n in back],
+        *[vmem((32, n), BF16) for n in back],
         vmem((2, 16, 128), F32),
         vmem((2, 32, 128), F32),
         vmem((2, 16, 128), F32),
@@ -981,6 +1008,8 @@
         pltpu.SemaphoreType.DMA((STEPS, 5)),
         pltpu.SemaphoreType.DMA((2,)),
         pltpu.SemaphoreType.DMA((STEPS, 2)),
+        pltpu.SemaphoreType.DMA((5,)),
+        pltpu.SemaphoreType.DMA((1, 5)),
         pltpu.SemaphoreType.DMA((5,)),
         pltpu.SemaphoreType.DMA((1, 5)),
         pltpu.SemaphoreType.DMA((2,)),

time: 67.4 us -> 65.7 us (0.975)
  Pallas kernels: 66.6 us -> 64.9 us
    pallas_call x1, Pallas kernels: 65.8 us -> 64.2 us  [on_device(): pl.pallas_call(functools.partial(kernel, bands, levs, loss_scale), out_sh...]
where the time goes in v4:
time: 65.7 us; the launch traced here: 65.6 us
  Pallas kernels  64.9 us (99%)
    pallas_call x1, Pallas kernels, on_device(): pl.pallas_call(functools.partial(kernel, bands, levs, loss_scale), out_sh...  64.2 us

profile of v4, /device:TPU:1, one launch (start us, length us, event | category | flops | bytes accessed | tf_op | source)
XLA Modules:
  0.0 65.6 jit_solution(14696653503267818321)
XLA Ops:
  0.6 64.2 %advection_step.1 = (f32[4,1,2,256]{3,2,1,0:T(2,128)S(1)}, f32[20,2,128]{2,1,0:T(2,128)S(1)}, f32[2,128]{1,0:T(2,128)S(1)}, f32[2,128,128]{2,1,0:T(8,128)S(1)}, ...) custom-call(f32[4,1,2,256]{3,2,1,0:T(2,128)} %conc_hbm.1, f32[4,1,2,256]{3,2,1,0:T(2,128)} %target_hbm.1, ...), custom_call_target="tpu_custom_call" | custom-call | tf_op jit(solution)/shard_map/advection_step/pallas_call | solution.py:1023
  64.8 0.7 %write_out.1 = (f32[4,1,2,256]{3,2,1,0:T(2,128)}, f32[20,2,128]{2,1,0:T(2,128)}, f32[2,128]{1,0:T(2,128)}, f32[2,128,128]{2,1,0:T(8,128)}, f32[2,128]{1,0:T(2,12...) custom-call(f32[4,1,2,256]{3,2,1,0:T(2,128)S(1)} %get-tuple-element.21.refs_0_, f32[20,2,128]{2,1,0:T(2,128)S(1)} %get-tuple-element.22.refs_1_, ...), custom_call_target="tpu_custom_call" | custom-call | tf_op jit(solution)/shard_map/write_out/pallas_call | solution.py:1035

commit v5 on v4

--- a/solution.py
+++ b/solution.py
@@ -411,14 +411,21 @@
     def quads(x, m, n):
         return (x[0:m, 0:n] + x[m : 2 * m, n : 2 * n]) + (x[0:m, n : 2 * n] + x[m : 2 * m, 0:n])
 
-    def weight_grads(net, s, lanes, ax, h2, d1, d2, pb):
+    def weight_stages(net, s, lanes, ax, h2, d1, d2, pb):
         out = dot_nt(ax[s, 0:288, lanes], d2[:, lanes])
+        yield
         grads[net * NET_ROWS : net * NET_ROWS + 128] += quads(out, 128, 128)
         accb2[net] += out[256:288, 0:128] + out[256:288, 128:256]
+        yield
         out = dot_nt(ax[s, 256:320, lanes], d1[:, lanes])
+        yield
         grads[net * NET_ROWS + 128 : (net + 1) * NET_ROWS] += quads(out, 32, 128)
         out = dot_nt(pb[:, lanes], h2[s, :, lanes])
+        yield
         acc3[net] += quads(out, 16, 128)
+
+    def weight_grads(*args):
+        run([weight_stages(*args)])
 
     def lane_fold(x):
         out = x[:, 0:128]
@@ -428,25 +435,37 @@
 
     zchunks = (slice(0, 256), slice(256, 512), slice(512, 640))
 
-    def zonal_stencil():
-        c = line[...]
-        return jnp.concatenate(
-            [pick(lane_roll(c, 1), c), pick(lane_roll(c, -1), lane_roll(c, -2))], 0
-        )
+    def zonal_many(parts):
+        stages = []
+        for at, which, c in parts:
+            stencil = jnp.concatenate(
+                [pick(lane_roll(c, 1), c), pick(lane_roll(c, -1), lane_roll(c, -2))], 0
+            )
+            for lanes in zchunks:
+                stages.append(
+                    forward(
+                        0,
+                        at,
+                        lanes,
+                        stencil[:, lanes],
+                        zcour[which, :, lanes],
+                        ax_z,
+                        h2_z,
+                        s1_z,
+                        s2_z,
+                        st_z,
+                        cf_z,
+                    )
+                )
+        fluxes = run(stages)
+        blocks = []
+        for i, (_, _, c) in enumerate(parts):
+            flux = jnp.concatenate(fluxes[3 * i : 3 * i + 3], 1)
+            blocks.append(pick(*from_line(c - (flux - lane_roll(flux, 1)))))
+        return blocks
 
     def zonal(s):
-        stencil = zonal_stencil()
-        parts = run(
-            [
-                forward(
-                    0, s, lanes, stencil[:, lanes], zcour[:, lanes], ax_z, h2_z, s1_z, s2_z, st_z, cf_z
-                )
-                for lanes in zchunks
-            ]
-        )
-        flux = jnp.concatenate(parts, 1)
-        new = line[...] - (flux - lane_roll(flux, 1))
-        return pick(*from_line(new))
+        return zonal_many([(s, 0, line[...])])[0]
 
     def face_stencil(s, face):
         mid = turn(halo[s, 2])
@@ -583,11 +602,11 @@
         rows = [ref[b, 0, r : r + 1, :] for r in range(2) for b in range(4)]
         return jnp.concatenate(rows, 0)
 
-    def zonal_constants(slab, steps):
+    def zonal_constants(slab, steps, which=0):
         zw = to_line(slab[4:5, :], slab[5:6, :])
         zs = to_line(slab[2:3, :], slab[3:4, :])
         courant = 0.5 * (zw + lane_roll(zw, -1))
-        zcour[...] = jnp.broadcast_to(courant, (8, NZ))
+        zcour[which] = jnp.broadcast_to(courant, (8, NZ))
         constant_rows(ax_z, 0, courant, zs, lane_roll(zs, -1), steps)
 
     def merid_constants(slots, steps):
@@ -619,8 +638,8 @@
         pl.semaphore_wait(barrier, greeted)
     move_start(block_out, halo, halo_send, halo_recv, (0, 1, 4))
     move_start(wind_out, winds, wind_send, wind_recv, (0, 1, 4))
+    move_start(wind_out, winds, wind_send, wind_recv, (2, 3))
     move_start(block_out, halo, halo_send, halo_recv, (2, 3))
-    move_start(wind_out, winds, wind_send, wind_recv, (2, 3))
     move_start(target_out, targets, target_send, target_recv, (0, 1, 4))
 
     @pl.when(moved)
@@ -642,6 +661,9 @@
         def _():
             zonal_constants(winds[0, 2], range(STEPS))
 
+    move_drain(block_out, halo, halo_send, halo_recv, (0, 1, 2, 3, 4))
+    zonal_constants(winds[0, 1], (STEPS,), 1)
+    zonal_constants(winds[0, 3], (STEPS + 1,), 2)
     with mark("waitmove"):
         move_wait(block_out, halo, halo_send, halo_recv, (0, 1, 4))
 
@@ -650,27 +672,44 @@
             f1, f2, f3 = merid_faces(s, (0, 1, 2))
             new = halo[s, 2] - pick(f2 - f1, f3 - f2)
             line[...] = to_line(*both_rows(new))
-        return new
-
-    move_drain(block_out, halo, halo_send, halo_recv, (0, 1, 2, 3, 4))
-    merid(0)
+
+    def merid_wide(s, own_flux):
+        with mark("merid4"):
+            f0, f4, f9, f5 = merid_faces(s, (3, 4, 5, 6))
+        f1, f2, f3 = own_flux
+        new = halo[s, 2] - pick(f2 - f1, f3 - f2)
+        before = halo[s, 1] - pick(f0 - f9, f1 - f0)
+        after = halo[s, 3] - pick(f4 - f3, f5 - f4)
+        return before, new, after
 
     def halo_step(s):
         with mark("zonal"):
             halo[s, 2] = zonal(s)
         halo_start(halo, s, halo_send, halo_recv, (0, 1, 2, 3))
 
-    halo_step(1)
-    with mark("redundant"):
+    with mark("merid"):
+        own_flux = merid_faces(0, (0, 1, 2))
+    with mark("waittwo"):
+        move_wait(wind_out, winds, wind_send, wind_recv, (2, 3))
+        merid_constants((5, 6), (0, STEPS - 1))
         move_wait(block_out, halo, halo_send, halo_recv, (2, 3))
-        merid_faces(0, (3, 4))
-        move_wait(wind_out, winds, wind_send, wind_recv, (2, 3))
-        merid_constants((5, 6), (STEPS - 1,))
-
-    with mark("waithalo"):
-        halo_wait(halo, 1, halo_send, halo_recv, (0, 1))
-    halo_drain(halo, 1, halo_send, halo_recv, (0, 1, 2, 3))
+    before, new, after = merid_wide(0, own_flux)
+    before = jnp.where(mine > 0, before, 0.0)
+    after = jnp.where(mine < bands - 1, after, 0.0)
+    with mark("zonal3"):
+        blocks = zonal_many(
+            [
+                (1, 0, to_line(*both_rows(new))),
+                (STEPS, 1, to_line(*both_rows(before))),
+                (STEPS + 1, 2, to_line(*both_rows(after))),
+            ]
+        )
+    halo[1, 2] = blocks[0]
+    halo_start(halo, 1, halo_send, halo_recv, (2, 3))
+    halo[1, 1] = blocks[1]
+    halo[1, 3] = blocks[2]
     merid(1)
+    halo_drain(halo, 1, halo_send, halo_recv, (2, 3))
     halo_step(2)
     with mark("redundant"):
         halo_wait(halo, 1, halo_send, halo_recv, (2, 3))
@@ -684,18 +723,14 @@
             zonal(0)
 
     move_wait(target_out, targets, target_send, target_recv, (0, 1, 4))
+    halo_drain(halo, 2, halo_send, halo_recv, (0, 1, 2, 3))
     with mark("waithalo"):
         halo_wait(halo, 2, halo_send, halo_recv, (0, 1))
-    halo_drain(halo, 2, halo_send, halo_recv, (0, 1, 2, 3))
     with mark("merid"):
-        f1, f2, f3 = merid_faces(2, (0, 1, 2))
+        own_flux = merid_faces(2, (0, 1, 2))
     with mark("waittwo"):
         halo_wait(halo, 2, halo_send, halo_recv, (2, 3))
-    with mark("merid4"):
-        f0, f4, f9, f5 = merid_faces(2, (3, 4, 5, 6))
-    new = halo[2, 2] - pick(f2 - f1, f3 - f2)
-    before = halo[2, 1] - pick(f0 - f9, f1 - f0)
-    after = halo[2, 3] - pick(f4 - f3, f5 - f4)
+    before, new, after = merid_wide(2, own_flux)
     ghalo[2, 2] = (new - targets[0, 2]) * loss_scale
     ghalo[2, 1] = jnp.where(mine > 0, (before - targets[0, 1]) * loss_scale, 0.0)
     ghalo[2, 3] = jnp.where(mine < bands - 1, (after - targets[0, 3]) * loss_scale, 0.0)
@@ -708,9 +743,9 @@
     def merid_back(s):
         @pl.when(s < STEPS - 1)
         def _():
+            halo_drain(ghalo, s, ghalo_send, ghalo_recv, (0, 1))
             with mark("waitg"):
                 halo_wait(ghalo, s, ghalo_send, ghalo_recv, (0, 1))
-            halo_drain(ghalo, s, ghalo_send, ghalo_recv, (0, 1))
 
         g = []
         for block in (1, 2, 3):
@@ -755,7 +790,7 @@
 
         gline[...] = to_line(*both_rows(new))
 
-    def zonal_back(s, last=False):
+    def zonal_back(s, last=False, beside=()):
         gz = gline[...]
         dflux = lane_roll(gz, -1) - gz
         outs = run(
@@ -765,7 +800,7 @@
                     s,
                     lanes,
                     dflux[:, lanes],
-                    zcour[:, lanes],
+                    zcour[0, :, lanes],
                     d1_z,
                     d2_z,
                     pb_z,
@@ -777,7 +812,8 @@
                 )
                 for lanes in zchunks
             ]
-        )
+            + list(beside)
+        )[: len(zchunks)]
         accp[0] += sum(lane_fold(o[1]) for o in outs)
         if last:
             return None
@@ -788,9 +824,10 @@
 
         return pick(*from_line(new))
 
-    def merid_weights(s):
-        weight_grads(1, s, slice(NY, 3 * NY), ax_m, h2_m, d1_m, d2_m, pb_m)
-
+    def inner_weights(s):
+        return weight_stages(1, s, slice(NY, 3 * NY), ax_m, h2_m, d1_m, d2_m, pb_m)
+
+    def first_face_weights(s):
         @pl.when(mine == 0)
         def _():
             weight_grads(1, s, slice(0, NY), ax_m, h2_m, d1_m, d2_m, pb_m)
@@ -804,30 +841,34 @@
         ghalo[s - 1, 2] = zonal_back(s)
         halo_start(ghalo, s - 1, ghalo_send, ghalo_recv, (0, 1))
         with mark("weights"):
-            merid_weights(s)
+            run([inner_weights(s)])
             zonal_weights(s)
+            first_face_weights(s)
         return carry
 
     lax.fori_loop(0, STEPS - 1, backward_step, 0)
 
-    centre = jnp.where(
-        lax.broadcasted_iota(jnp.int32, (16, 16), 1) // 4
-        == lax.broadcasted_iota(jnp.int32, (16, 16), 0),
-        0.75,
-        -0.25,
-    )
-    centre = jnp.concatenate([centre, centre], 1).astype(BF16)
+    def groups(x):
+        x = x + pltpu.roll(x, 7, axis=0)
+        return x + pltpu.roll(x, 6, axis=0)
 
     def gather_net(net):
         top = net * NET_ROWS
         grads[top + 149 : top + 150] = accb2[net, 20:21, :]
-        grads[top + 152 : top + 156] = dot(centre, stack(acc3[net]))[0:4]
+        low, high = groups(acc3[net, 0:8]), groups(acc3[net, 8:16])
+        rows = [low[0:1], low[4:5], high[0:1], high[4:5]]
+        middle = 0.25 * ((rows[0] + rows[1]) + (rows[2] + rows[3]))
+        for j in range(4):
+            grads[top + 152 + j : top + 153 + j] = rows[j] - middle
+
+    def gather_bias(net):
         sums = jnp.sum(accp[net], 1, keepdims=True)
-        mine = (
+        own = (
             lax.broadcasted_iota(jnp.int32, (16, WIDTH), 0) // 4
             == lax.broadcasted_iota(jnp.int32, (16, WIDTH), 1)
         )
-        row = jnp.sum(jnp.where(mine, sums, 0.0), 0, keepdims=True)
+        row = jnp.sum(jnp.where(own, sums, 0.0), 0, keepdims=True)
+        top = net * NET_ROWS
         grads[top + 156 : top + 157] = row - jnp.sum(row, 1, keepdims=True) * 0.25
 
     piece = GRAD_ROWS // levs
@@ -876,13 +917,15 @@
             first_copy(net, 0).start()
 
     merid_back(0)
+    with mark("zback0"):
+        zonal_back(0, True, [inner_weights(0)])
     with mark("wg1"):
-        merid_weights(0)
+        first_face_weights(0)
     with mark("gather1"):
+        gather_bias(1)
+        gather_bias(0)
         gather_net(1)
         send_net(1)
-    with mark("zback0"):
-        zonal_back(0, True)
     with mark("wg0"):
         zonal_weights(0)
     with mark("gather0"):
@@ -955,7 +998,7 @@
     side_z = bands // side_y
     part = piece // side_y
     vmem = pltpu.VMEM
-    sweeps = [NZ, NM]
+    saved = [(STEPS + 2, NZ), (STEPS, NM)]
     back = [NZ, NB]
     args = list(args)
     args[5] = jnp.transpose(args[5], (1, 0, 2))
@@ -970,7 +1013,7 @@
         vmem((2, 32, 256), BF16),
         vmem((2, 128, 128), F32),
         vmem((2, 16, 128), F32),
-        vmem((8, NZ), F32),
+        vmem((3, 8, NZ), F32),
         vmem((8, NM), F32),
         vmem((STEPS, 5, 8, NY), F32),
         vmem((STEPS, 5, 8, NY), F32),
@@ -985,12 +1028,12 @@
         vmem((8, NY), F32),
         vmem((8, NZ), F32),
         vmem((8, NZ), F32),
-        *[vmem((STEPS, 352, n), BF16) for n in sweeps],
-        *[vmem((STEPS, 256, n), BF16) for n in sweeps],
-        *[vmem((STEPS, 128, n), F32) for n in sweeps],
-        *[vmem((STEPS, 128, n), F32) for n in sweeps],
-        *[vmem((STEPS, 16, n), F32) for n in sweeps],
-        *[vmem((STEPS, 16, n), F32) for n in sweeps],
+        *[vmem((k, 352, n), BF16) for k, n in saved],
+        *[vmem((k, 256, n), BF16) for k, n in saved],
+        *[vmem((k, 128, n), F32) for k, n in saved],
+        *[vmem((k, 128, n), F32) for k, n in saved],
+        *[vmem((k, 16, n), F32) for k, n in saved],
+        *[vmem((k, 16, n), F32) for k, n in saved],
         *[vmem((256, n), BF16) for n in back],
         *[vmem((256, n), BF16) for n in back],
         *[vmem((32, n), BF16) for n in back],

time: 65.7 us -> 64.4 us (0.980)
  Pallas kernels: 64.9 us -> 63.6 us
    pallas_call x1, Pallas kernels: 64.2 us -> 62.8 us  [on_device(): pl.pallas_call(functools.partial(kernel, bands, levs, loss_scale), out_sh...]
where the time goes in v5:
time: 64.4 us; the launch traced here: 64.2 us
  Pallas kernels  63.6 us (99%)
    pallas_call x1, Pallas kernels, on_device(): pl.pallas_call(functools.partial(kernel, bands, levs, loss_scale), out_sh...  62.8 us

profile of v5, /device:TPU:1, one launch (start us, length us, event | category | flops | bytes accessed | tf_op | source)
XLA Modules:
  0.0 64.2 jit_solution(3894432834279987822)
XLA Ops:
  0.6 62.8 %advection_step.1 = (f32[4,1,2,256]{3,2,1,0:T(2,128)S(1)}, f32[20,2,128]{2,1,0:T(2,128)S(1)}, f32[2,128]{1,0:T(2,128)S(1)}, f32[2,128,128]{2,1,0:T(8,128)S(1)}, ...) custom-call(f32[4,1,2,256]{3,2,1,0:T(2,128)} %conc_hbm.1, f32[4,1,2,256]{3,2,1,0:T(2,128)} %target_hbm.1, ...), custom_call_target="tpu_custom_call" | custom-call | tf_op jit(solution)/shard_map/advection_step/pallas_call | solution.py:1066
  63.5 0.7 %write_out.1 = (f32[4,1,2,256]{3,2,1,0:T(2,128)}, f32[20,2,128]{2,1,0:T(2,128)}, f32[2,128]{1,0:T(2,128)}, f32[2,128,128]{2,1,0:T(8,128)}, f32[2,128]{1,0:T(2,12...) custom-call(f32[4,1,2,256]{3,2,1,0:T(2,128)S(1)} %get-tuple-element.21.refs_0_, f32[20,2,128]{2,1,0:T(2,128)S(1)} %get-tuple-element.22.refs_1_, ...), custom_call_target="tpu_custom_call" | custom-call | tf_op jit(solution)/shard_map/write_out/pallas_call | solution.py:1078
